TPU v7x, 128 devices: a whole 4x4x4 slice. The times are simulated.
128 devices in a mesh: src: 32 (over y, x_hi, z), sta: 4 (over x_lo, core).
Axes of the slice: x: 4 (x_hi: 2, x_lo: 2; x = x_hi * 2 + x_lo), y: 4, z: 4, core: 2. Of those that a mesh axis runs over, the one named last changes fastest.
Arguments:
- trace: float32 [256, 8256], P('sta', 'src'), may hold values from -6 to 6
- quadrature: float32 [256, 8256], P('sta', 'src'), may hold values from -6 to 6
- gains: float32 [256], P('sta'), may hold values from 0.3 to 3
- lags: int32 [4096, 256], P('src', 'sta'), may hold values from 0 to 63
Outputs:
- beam_power: float32 [2, 4096], P(None, 'src')
All inputs are finite; a program needn't handle non-finite values.
Results may differ from a plain program's by a relative error of at most 0.0003.
Values may be sent and summed in bfloat16 or wider, within the bound.
No kernel may reach another device: no remote copies, remote signals or barrier semaphores. Data moves between devices by JAX's collectives and lax.ppermute only.
A program may use at most 256 MiB of HBM per device.

v0:
```python
import jax
import jax.numpy as jnp
from jax import lax
from jax.sharding import PartitionSpec as P

W = 4096
LAGS = 64
STEPS = 2


def on_device(trace, quadrature, gains, lags):
    energy = trace * trace + quadrature * quadrature
    row_totals = lax.psum(jnp.sum(energy, axis=1), "src")
    baseline = row_totals / (energy.shape[1] * lax.axis_size("src"))
    weighted = (gains[:, None] * (energy - baseline[:, None])).astype(jnp.bfloat16)
    envelope = lax.all_gather(weighted, "src", axis=1, tiled=True)
    cell_count, station_count = lags.shape
    offsets = jnp.arange(LAGS, dtype=jnp.int32)
    selector = (lags[:, None, :] == offsets[None, :, None]).astype(jnp.bfloat16)
    selector = selector.reshape(cell_count, LAGS * station_count)
    power_rows = []
    for step_index in range(STEPS):
        start = step_index * W
        stacked = jnp.concatenate(
            [envelope[:, start + lag_index : start + lag_index + W] for lag_index in range(LAGS)],
            axis=0,
        )
        partial_beam = jnp.dot(selector, stacked, preferred_element_type=jnp.float32)
        beam = lax.psum(partial_beam, "sta")
        power_rows.append(jnp.sum(beam * beam, axis=1))
    power = jnp.stack(power_rows)
    peak_power = lax.pmax(jnp.max(power, axis=1), "src")
    return power / peak_power[:, None]


def solution(mesh):
    return jax.shard_map(
        on_device,
        mesh=mesh,
        in_specs=(P("sta", "src"), P("sta", "src"), P("sta"), P("src", "sta")),
        out_specs=P(None, "src"),
        check_vma=False,
    )
```

profile of v0, /device:TPU:0, one launch (start us, length us, event | category | flops | bytes accessed | tf_op | source)
XLA Modules:
  0.0 483.9 jit_solution(4156925438073581276)
XLA Ops:
  7.6 97.9 %psum.21 = f32[64]{0:T(128)S(1)} all-reduce(f32[64]{0:T(128)S(1)} %fusion.1), channel_id=1, replica_groups=mesh['src'=32,'sta'=4] {'src'}, use_global_device_ids=true, to_apply=%region_1.0 | all-reduce | flops 64 | bytes 512 | tf_op jit(solution)/shard_map/psum | solution.py:13
  105.5 1.7 fusion
  107.3 1.5 bitcast_compare_fusion
  108.8 61.0 %all-gather.3.cloned.1.call-done = bf16[32,258,64]{1,2,0:T(8,128)(2,1)} async-done(((bf16[1,258,64]{1,2,0:T(8,128)(2,1)}), bf16[32,258,64]{1,2,0:T(8,128)(2,1)}) %all-gather.3.cloned.1.call-update) | async-done | bytes 1056784 | tf_op jit(solution)/shard_map/all_gather | solution.py:16
  169.9 2.3 copy.7
  172.2 1.9 reshape.8
  176.1 1.2 slice_dynamic-update-slice_fusion.125
  190.1 1.2 slice_dynamic-update-slice_fusion.113
  191.3 1.2 slice_dynamic-update-slice_fusion.112
  192.5 1.2 slice_dynamic-update-slice_fusion.111
  194.9 1.2 slice_dynamic-update-slice_fusion.109
  200.7 1.2 slice_dynamic-update-slice_fusion.104
  212.4 1.4 slice_dynamic-update-slice_fusion.94
  223.1 1.2 slice_dynamic-update-slice_fusion.85
  227.7 1.2 slice_dynamic-update-slice_fusion.81
  228.9 1.2 slice_dynamic-update-slice_fusion.80
  232.5 1.2 slice_dynamic-update-slice_fusion.77
  238.3 1.2 slice_dynamic-update-slice_fusion.72
  248.8 11.1 %copy-done = bf16[4096,4096]{1,0:T(8,128)(2,1)} copy-done((bf16[4096,4096]{1,0:T(8,128)(2,1)}, bf16[4096,4096]{1,0:T(8,128)(2,1)S(1)}, u32[]{:S(2)}) %copy-start) | copy-done | bytes 33554456
  259.9 14.4 %fusion.3 = f32[128,4096]{1,0:T(8,128)} fusion(pred[128,4096]{0,1:T(32,128)(4,1)S(1)} %bitcast_compare_fusion, bf16[4096,4096]{1,0:T(8,128)(2,1)} %copy-done), kind=kOutput, calls=%fused_computation.139 | convolution fusion | flops 4294967296 | bytes 36175872 | tf_op jit(solution)/shard_map/dot_general | solution.py:28
  274.3 14.3 %fusion.4 = f32[128,4096]{1,0:T(8,128)} fusion(pred[128,4096]{0,1:T(32,128)(4,1)S(1)} %bitcast_compare_fusion, bf16[4096,4096]{1,0:T(8,128)(2,1)} %get-tuple-element.8), kind=kOutput, calls=%fused_computation.140 | convolution fusion | flops 4294967296 | bytes 36175872 | tf_op jit(solution)/shard_map/dot_general | solution.py:28
  288.6 89.0 %all-reduce.3.cloned.1.call-done = (f32[128,4096]{1,0:T(8,128)}, f32[128,4096]{1,0:T(8,128)}) async-done(((f32[128,4096]{1,0:T(8,128)}, f32[128,4096]{1,0:T(8,128)}), (f32[128,4096]{1,0:T(8,128)}, f32[128,4096]{1,0:T(8,128)})) %all-reduce.3.cloned.1.call-update) | async-done | bytes 4194320 | tf_op jit(solution)/shard_map/psum | solution.py:29
  377.6 2.6 multiply_reduce_fusion
  380.3 96.1 %pmax.7 = f32[2]{0:T(128)S(1)} all-reduce(f32[2]{0:T(128)S(1)} %fusion.2), channel_id=1, replica_groups=mesh['src'=32,'sta'=4] {'src'}, use_global_device_ids=true, to_apply=%region_7.0 | all-reduce | flops 2 | bytes 16 | tf_op jit(solution)/shard_map/pmax | solution.py:32
  (63 shorter events, 62.2 us)
Async XLA Ops:
  6.5 163.3 %all-gather.3.cloned.1.call-start = ((), (), s32[]{:S(2)}) async-start(), calls=%async_computation | async-start | bytes 1622016 | tf_op jit(solution)/shard_map/all_gather | solution.py:16
  107.2 270.4 %all-reduce.3.cloned.1.call-start = ((), (), s32[]{:S(2)}) async-start(), calls=%async_computation.1 | async-start | bytes 8388608 | tf_op jit(solution)/shard_map/psum | solution.py:29
  248.8 11.1 %copy-start = (bf16[4096,4096]{1,0:T(8,128)(2,1)}, bf16[4096,4096]{1,0:T(8,128)(2,1)S(1)}, u32[]{:S(2)}) copy-start(bf16[4096,4096]{1,0:T(8,128)(2,1)S(1)} %get-tuple-element.7) | copy-start | bytes 100663296
Sparse Core Ops, SparseCore 0:
  107.3 62.4 all-gather.2
  288.8 88.8 all-reduce.2
where the time goes:
time: 484 us
  blocking collectives  194 us (40%)
  waiting for transfers between devices  150 us (31%)
  local copies, waits for them, and re-layouts  90.1 us (19%)
  matrix products  28.7 us (6%)
  between operations  13.5 us (3%)
  other arithmetic  7.54 us (2%)
    psum x1, blocking collectives, on_device(): row_totals = lax.psum(jnp.sum(energy, axis=1), 'src')  97.9 us
    pmax x1, blocking collectives, on_device(): peak_power = lax.pmax(jnp.max(power, axis=1), 'src')  96.1 us
    psum x1, waiting for transfers between devices, on_device(): beam = lax.psum(partial_beam, 'sta')  89 us
    unnamed x66, local copies, waits for them, and re-layouts  86.5 us
    all_gather x1, waiting for transfers between devices, on_device(): envelope = lax.all_gather(weighted, 'src', axis=1, tiled=True)  61 us
    dot_general x2, matrix products, on_device(): jnp.dot(selector, stacked, preferred_element_type=jnp.float32)  28.7 us
  transfers between devices with their start and end apart: 2, of which 2 were waited for; matrix products, arithmetic and copies ran while one was open for 0% of the time, Pallas kernels for 0%

commit v1 on v0

v1 whole, which is shorter than its diff:
```python
import functools

import jax
import jax.numpy as jnp
from jax import lax
from jax.experimental import pallas as pl
from jax.experimental.pallas import tpu as pltpu
from jax.sharding import PartitionSpec as P

W = 4096
LAGS = 64
STEPS = 2
F32 = jnp.float32
BF16 = jnp.bfloat16
VMEM = pl.BlockSpec(memory_space=pltpu.VMEM)
SMEM = pl.BlockSpec(memory_space=pltpu.SMEM)

SRC = 32
STA = 4
DEV = SRC * STA
BLK = 258
ST = 64
STATIONS = ST * STA
WIN = 256
CPD = 128
ROWS = 24
SAMPLES = BLK * SRC
HALF = SRC // STEPS * STA


def prologue(where, trace, quad, gains, lags, own, left, right, chunk):
    tr, qd = trace[...], quad[...]
    energy = tr * tr + qd * qd
    own[:, :BLK] = energy
    own[:, BLK:] = jnp.broadcast_to(gains[...], (ST, 384 - BLK))
    left[...] = energy[:, BLK - 128 :]
    right[...] = energy[:, :128]
    total = jnp.sum(energy, axis=1, keepdims=True)
    total = jnp.broadcast_to(total, (ST, 128))
    total = jnp.concatenate([total, total], axis=0).T[:8]
    hi = total.astype(BF16).astype(F32)
    mid = (total - hi).astype(BF16).astype(F32)
    low = total - hi - mid
    row = lax.broadcasted_iota(jnp.int32, (8, 128), 0)
    lane = lax.broadcasted_iota(jnp.int32, (8, 128), 1)
    sums = jnp.where(row == 0, hi, jnp.where(row == 1, mid, jnp.where(row == 2, low, 0.0)))
    sums = jnp.where(lane // ST == where[1] % 2, sums, 0.0)
    for j in range(STA):
        first = lags[32 * j : 32 * j + 16, :]
        second = lags[32 * j + 16 : 32 * j + 32, :]
        body = jnp.concatenate([first, second], axis=1).astype(F32)
        chunk[j] = jnp.concatenate([body, sums], axis=0).astype(BF16)


def window(where, e0, e1, e2, e3, h0, h1, h2, h3, win, gains, tall, edges, line):
    for k, (e, h) in enumerate(((e0, h0), (e1, h1), (e2, h2), (e3, h3))):
        at = pl.multiple_of((where[1] + k) % STA * ST, ST)
        tall[pl.ds(at, ST), :] = e[...]
        edges[pl.ds(at, ST), :] = h[...]
    side = edges[...].T
    main = tall[...].T
    line[64:448, :] = main
    line[0:64, :] = side[64:128]
    line[64 + BLK : 64 + BLK + 64, :] = side[0:64]
    win[...] = pltpu.roll(line[...], 448 - 64 + 2 * where[0], 0)[:320]
    gains[...] = jnp.broadcast_to(main[BLK : BLK + 1], (8, STATIONS))


def beams(received, win, gains, power, weighted, lagged):
    halves = []
    for half in range(2):
        acc = jnp.zeros((8, 128), F32)
        for i in range(SRC):
            for j in (2 * half, 2 * half + 1):
                acc = acc + received[STA * i + j, 16:24, :].astype(F32)
        halves.append(jnp.sum(acc, axis=0, keepdims=True))
    baseline = jnp.concatenate(halves, axis=1) / SAMPLES
    gain = gains[0:1, :]
    for b in range(16):
        rows = 304 if b < 15 else 304
        weighted[b] = (gain * (win[b : b + rows, :] - baseline)).astype(BF16)
    for j in range(STA):
        part = jnp.concatenate([received[STA * i + j, 0:16, :] for i in range(SRC)], axis=0)
        part = part.astype(F32).T.astype(BF16)
        for h in range(2):
            lagged[h, ST * j : ST * j + ST, :] = part[ST * h : ST * h + ST]
    for group in range(4):
        cols = slice(256 * (group % 2), 256 * (group % 2) + 256)

        def add(step, total):
            base = pl.multiple_of(step * 16, 16)
            picks, shifted = [], []
            lag = lagged[group // 2, :, cols]
            for b in range(16):
                value = (base + b).astype(F32).astype(BF16)
                picks.append(jnp.where(lag == value, BF16(1), BF16(0)))
                shifted.append(weighted[b, pl.ds(base, WIN), :])
            return total + jnp.dot(
                jnp.concatenate(shifted, axis=1), jnp.concatenate(picks, axis=0), preferred_element_type=F32
            )

        beam = lax.fori_loop(0, LAGS // 16, add, jnp.zeros((WIN, 256), F32))
        squared = jnp.sum(beam * beam, axis=0, keepdims=True)
        power[2 * group : 2 * group + 1, :] = squared[:, :128]
        power[2 * group + 1 : 2 * group + 2, :] = squared[:, 128:]


def finish(where, parts, out, sums):
    src = where[0]
    lane = lax.broadcasted_iota(jnp.int32, (1, 128), 1)
    for k in range(STEPS):
        peak = None
        for j in range(STA):
            acc = parts[k * HALF + j]
            for i in range(1, SRC // STEPS):
                acc = acc + parts[k * HALF + STA * i + j]
            sums[8 * j : 8 * j + 8, :] = acc
            peak = acc if peak is None else jnp.maximum(peak, acc)
        peak = jnp.max(peak, axis=(0, 1), keepdims=True)
        cells = jnp.zeros((1, 128), F32)
        for j in range(STA):
            for h in range(2):
                row = sums[pl.ds(8 * j + 4 * h + src // 8, 1), :]
                to = 32 * j + 16 * h
                row = pltpu.roll(row, (to - 16 * (src % 8)) % 128, 1)
                cells = jnp.where(lane // 16 == to // 16, row, cells)
        out[k : k + 1, :] = cells / peak


def call(kernel, out_shape, specs, scratch=(), name=None):
    multi = isinstance(out_shape, (list, tuple))
    return pl.pallas_call(
        kernel,
        out_shape=out_shape,
        in_specs=specs,
        out_specs=[VMEM] * len(out_shape) if multi else VMEM,
        scratch_shapes=scratch,
        compiler_params=pltpu.CompilerParams(vmem_limit_bytes=48 << 20),
        name=name,
    )


def shape(dims, dtype=F32):
    return jax.ShapeDtypeStruct(dims, dtype)


def on_device(trace, quadrature, gains, lags):
    where = jnp.stack([lax.axis_index("src"), lax.axis_index("sta")]).astype(jnp.int32)
    own, left, right, chunk = call(
        prologue,
        [shape((ST, 384)), shape((ST, 128)), shape((ST, 128)), shape((STA, ROWS, 128), BF16)],
        [SMEM] + [VMEM] * 4,
        name="prologue",
    )(where, trace, quadrature, gains[:, None], lags)
    chunks = jnp.broadcast_to(chunk[None], (SRC, STA, ROWS, 128)).reshape(DEV, ROWS, 128)
    received = lax.all_to_all(chunks, ("src", "sta"), 0, 0, tiled=True)

    def from_sta(x, k):
        return lax.ppermute(x, "sta", [((j + k) % STA, j) for j in range(STA)])

    blocks = [own] + [from_sta(own, k) for k in range(1, STA)]
    before = lax.ppermute(left, "src", [(i, (i + 1) % SRC) for i in range(SRC)])
    after = lax.ppermute(right, "src", [((i + 1) % SRC, i) for i in range(SRC)])
    edge = jnp.where(jnp.arange(128)[None, :] < 64, after, before)
    edges = [edge] + [from_sta(edge, k) for k in range(1, STA)]
    win, gain = call(
        window,
        [shape((320, STATIONS)), shape((8, STATIONS))],
        [SMEM] + [VMEM] * 8,
        [pltpu.VMEM((STATIONS, 384), F32), pltpu.VMEM((STATIONS, 128), F32), pltpu.VMEM((448, STATIONS), F32)],
        name="window",
    )(where, *blocks, *edges)
    power = call(
        beams,
        shape((8, 128)),
        [VMEM] * 3,
        [pltpu.VMEM((16, 304, STATIONS), BF16), pltpu.VMEM((2, STATIONS, 512), BF16)],
        name="beams",
    )(received, win, gain)
    parts = lax.all_to_all(jnp.broadcast_to(power[None], (DEV, 8, 128)), ("src", "sta"), 0, 0, tiled=True)
    return call(finish, shape((STEPS, CPD)), [SMEM, VMEM], [pltpu.VMEM((32, 128), F32)], name="finish")(where, parts)


def solution(mesh):
    return jax.shard_map(
        on_device,
        mesh=mesh,
        in_specs=(P("sta", "src"), P("sta", "src"), P("sta"), P("src", "sta")),
        out_specs=P(None, "src"),
        check_vma=False,
    )
```

time: 484 us -> 74.7 us (0.15)
  blocking collectives: 194 us -> 17.5 us
  waiting for transfers between devices: 150 us -> 15.2 us
  local copies, waits for them, and re-layouts: 90.1 us -> 2.83 us
  matrix products: 28.7 us -> 0 us
  starting transfers between devices: 0.04 us -> 22.4 us
  Pallas kernels: 0 us -> 15.7 us
  between operations: 13.5 us -> 0.06 us
  other arithmetic: 7.54 us -> 0.09 us
    psum x1 -> x0, blocking collectives: 97.9 us -> none  [on_device(): row_totals = lax.psum(jnp.sum(energy, axis=1), 'src')]
    pmax x1 -> x0, blocking collectives: 96.1 us -> none  [on_device(): peak_power = lax.pmax(jnp.max(power, axis=1), 'src')]
    psum x1 -> x0, waiting for transfers between devices: 89 us -> none  [on_device(): beam = lax.psum(partial_beam, 'sta')]
    unnamed x66 -> x7, local copies, waits for them, and re-layouts: 86.5 us -> 0.99 us
    all_gather x1 -> x0, waiting for transfers between devices: 61 us -> none  [on_device(): envelope = lax.all_gather(weighted, 'src', axis=1, tiled=True)]
    dot_general x2 -> x0, matrix products: 28.7 us -> none  [on_device(): jnp.dot(selector, stacked, preferred_element_type=jnp.float32)]
    all_to_all x0 -> x1, blocking collectives: none -> 17.5 us  [on_device(): lax.all_to_all(jnp.broadcast_to(power[None], (DEV, 8, 128)), ('src', 'sta...]
    pallas_call x0 -> x4, Pallas kernels: none -> 15.7 us  [the longest x1 12.9 us: on_device(): call(beams, shape((8, 128)), [VMEM] * 3, [pltpu.VMEM((16, 304, STATIONS),...]
  transfers between devices with their start and end apart: 2 -> 9, of which waited for: 2 -> 5; matrix products, arithmetic and copies ran while one was open for 0% -> 0% of each run, Pallas kernels for 0% -> 1%
where the time goes in v1:
time: 74.7 us; the launch traced here: 73.7 us
  starting transfers between devices  22.4 us (30%)
  blocking collectives  17.5 us (23%)
  Pallas kernels  15.7 us (21%)
  waiting for transfers between devices  15.2 us (20%)
  local copies, waits for them, and re-layouts  2.83 us (4%)
    all_to_all x1, blocking collectives, on_device(): lax.all_to_all(jnp.broadcast_to(power[None], (DEV, 8, 128)), ('src', 'sta...  17.5 us
    pallas_call x1, Pallas kernels, on_device(): call(beams, shape((8, 128)), [VMEM] * 3, [pltpu.VMEM((16, 304, STATIONS),...  12.9 us
    all_to_all x1, starting transfers between devices, on_device(): received = lax.all_to_all(chunks, ('src', 'sta'), 0, 0, tiled=True)  11.2 us
    ppermute x1, waiting for transfers between devices, on_device(): before = lax.ppermute(left, 'src', [(i, (i + 1) % SRC) for i in range(SRC)])  8.71 us
    ppermute x1, starting transfers between devices, on_device(): after = lax.ppermute(right, 'src', [((i + 1) % SRC, i) for i in range(SRC)])  8.15 us
    ppermute x6, waiting for transfers between devices, from_sta(): return lax.ppermute(x, 'sta', [((j + k) % STA, j) for j in range(STA)])  3.37 us
    ppermute x1, waiting for transfers between devices, on_device(): after = lax.ppermute(right, 'src', [((i + 1) % SRC, i) for i in range(SRC)])  3.1 us
    ppermute x6, starting transfers between devices, from_sta(): return lax.ppermute(x, 'sta', [((j + k) % STA, j) for j in range(STA)])  3.05 us
  transfers between devices with their start and end apart: 9, of which 5 were waited for; matrix products, arithmetic and copies ran while one was open for 0% of the time, Pallas kernels for 1%

profile of v1, /device:TPU:0, one launch (start us, length us, event | category | flops | bytes accessed | tf_op | source)
XLA Modules:
  0.0 73.7 jit_solution(2554371285817031964)
XLA Ops:
  0.0 0.8 %copy.5.gains = f32[64,1]{1,0:T(8,128)S(1)} copy(f32[64,1]{0,1:T(1,128)} %bitcast.4) | data formatting | bytes 512 | tf_op jit(solution)/shard_map/broadcast_in_dim | solution.py:154
  0.8 0.1 copy.6.lags
  0.9 0.1 pad_add_fusion.where
  1.0 0.9 %copy-done.1 = f32[64,258]{1,0:T(8,128)S(1)} copy-done((f32[64,258]{1,0:T(8,128)S(1)}, f32[64,258]{1,0:T(8,128)}, u32[]{:S(2)}) %copy-start.1) | copy-done | bytes 66072
  1.9 0.7 prologue.1
  2.6 1.0 %broadcast_in_dim.15 = bf16[32,4,24,128]{3,2,1,0:T(8,128)(2,1)} broadcast(bf16[4,24,128]{2,1,0:T(8,128)(2,1)S(1)} %get-tuple-element.11), dimensions={1,2,3} | broadcast | bytes 811008 | tf_op jit(solution)/shard_map/broadcast_in_dim | solution.py:155
  3.6 11.2 %all-to-all-start = ((bf16[128,24,128]{2,1,0:T(8,128)(2,1)}), bf16[128,24,128]{2,1,0:T(8,128)(2,1)S(1)}, u32[]{:S(2)}, u32[]{:S(2)}) async-start(bf16[128,24,128]{2,1,0:T(8,128)(2,1)} %bitcast.3), calls=%async_computation | async-start | bytes 1572864 | tf_op jit(solution)/shard_map/all_to_all | solution.py:156
  14.8 0.7 %collective-permute-start = (f32[64,384]{1,0:T(8,128)S(1)}, f32[64,384]{1,0:T(8,128)S(1)}, u32[]{:S(2)}, u32[]{:S(2)}) collective-permute-start(f32[64,384]{1,0:T(8,128)S(1)} %get-tuple-element.12.e0), channel_id=1, source_target_pairs={{1,0},{2,1},{3,2},{0,3},{5,4},{6,5},{7,6},{4,7},{9,8},{10,9},{11,1... | collective-permute-start | bytes 294920 | tf_op jit(solution)/shard_map/ppermute | solution.py:159
  15.5 0.4 collective-permute-start.1
  15.9 0.1 collective-permute-start.2
  16.0 8.1 %collective-permute-start.3 = (f32[64,128]{1,0:T(8,128)S(1)}, f32[64,128]{1,0:T(8,128)S(1)}, u32[]{:S(2)}, u32[]{:S(2)}) collective-permute-start(f32[64,128]{1,0:T(8,128)S(1)} %get-tuple-element.13), channel_id=1, source_target_pairs={{4,0},{8,4},{12,8},{16,12},{20,16},{24,20},{28,24},{32,28},{36,32}... | collective-permute-start | bytes 98312 | tf_op jit(solution)/shard_map/ppermute | solution.py:163
  24.2 0.0 collective-permute-start.4
  24.2 3.1 %collective-permute-done.3 = f32[64,128]{1,0:T(8,128)S(1)} collective-permute-done((f32[64,128]{1,0:T(8,128)S(1)}, f32[64,128]{1,0:T(8,128)S(1)}, u32[]{:S(2)}, u32[]{:S(2)}) %collective-permute-start.3) | collective-permute-done | bytes 32800 | tf_op jit(solution)/shard_map/ppermute | solution.py:163
  27.3 8.7 %collective-permute-done.4 = f32[64,128]{1,0:T(8,128)S(1)} collective-permute-done((f32[64,128]{1,0:T(8,128)S(1)}, f32[64,128]{1,0:T(8,128)S(1)}, u32[]{:S(2)}, u32[]{:S(2)}) %collective-permute-start.4) | collective-permute-done | bytes 32800 | tf_op jit(solution)/shard_map/ppermute | solution.py:162
  36.0 0.0 collective-permute-start.5
  36.0 0.9 %collective-permute-start.6 = (f32[64,128]{1,0:T(8,128)S(1)}, f32[64,128]{1,0:T(8,128)S(1)}, u32[]{:S(2)}, u32[]{:S(2)}) collective-permute-start(f32[64,128]{1,0:T(8,128)S(1)} %broadcast_select_fusion.h0), channel_id=1, source_target_pairs={{2,0},{3,1},{0,2},{1,3},{6,4},{7,5},{4,6},{5,7},{10,8},{11,9},{8,1... | collective-permute-start | bytes 98312 | tf_op jit(solution)/shard_map/ppermute | solution.py:159
  36.9 0.8 %collective-permute-done.5.h1 = f32[64,128]{1,0:T(8,128)S(1)} collective-permute-done((f32[64,128]{1,0:T(8,128)S(1)}, f32[64,128]{1,0:T(8,128)S(1)}, u32[]{:S(2)}, u32[]{:S(2)}) %collective-permute-start.5) | collective-permute-done | bytes 32800 | tf_op jit(solution)/shard_map/ppermute | solution.py:159
  37.7 0.9 %collective-permute-start.7 = (f32[64,128]{1,0:T(8,128)S(1)}, f32[64,128]{1,0:T(8,128)S(1)}, u32[]{:S(2)}, u32[]{:S(2)}) collective-permute-start(f32[64,128]{1,0:T(8,128)S(1)} %broadcast_select_fusion.h0), channel_id=1, source_target_pairs={{3,0},{0,1},{1,2},{2,3},{7,4},{4,5},{5,6},{6,7},{11,8},{8,9},{9,10... | collective-permute-start | bytes 98312 | tf_op jit(solution)/shard_map/ppermute | solution.py:159
  38.6 1.4 %collective-permute-done.6.h2 = f32[64,128]{1,0:T(8,128)S(1)} collective-permute-done((f32[64,128]{1,0:T(8,128)S(1)}, f32[64,128]{1,0:T(8,128)S(1)}, u32[]{:S(2)}, u32[]{:S(2)}) %collective-permute-start.6) | collective-permute-done | bytes 32800 | tf_op jit(solution)/shard_map/ppermute | solution.py:159
  40.0 1.2 %collective-permute-done.7.h3 = f32[64,128]{1,0:T(8,128)S(1)} collective-permute-done((f32[64,128]{1,0:T(8,128)S(1)}, f32[64,128]{1,0:T(8,128)S(1)}, u32[]{:S(2)}, u32[]{:S(2)}) %collective-permute-start.7) | collective-permute-done | bytes 32800 | tf_op jit(solution)/shard_map/ppermute | solution.py:159
  41.2 0.8 %window.1 = (f32[320,256]{1,0:T(8,128)S(1)}, f32[8,256]{1,0:T(8,128)S(1)}) custom-call(s32[2]{0:T(128)S(1)} %pad_add_fusion.where, f32[64,384]{1,0:T(8,128)S(1)} %get-tuple-element.12.e0, f32[64,384]{1,0:T(8,128)S(1)} %collective-permute-done.e1, f32[64,384]{1,0:T(8,128)S(1)} %collective-permute-done.1.e2, f32[64,384]{1,0:T(8,128)S(1)} %collective-permute-done.2.e3, ...), custom_call_target="tpu_custom_call" | custom-call | tf_op jit(solution)/shard_map/window/pallas_call | solution.py:166
  42.0 12.9 %beams.1 = f32[8,128]{1,0:T(8,128)S(1)} custom-call(bf16[128,24,128]{2,1,0:T(8,128)(2,1)S(1)} %all-to-all-done.received, f32[320,256]{1,0:T(8,128)S(1)} %get-tuple-element.15.win, f32[8,256]{1,0:T(8,128)S(1)} %get-tuple-element.16.gains), custom_call_target="tpu_custom_call" | custom-call | tf_op jit(solution)/shard_map/beams/pallas_call | solution.py:173
  55.0 17.5 %all_to_all.10.parts = f32[128,8,128]{2,1,0:T(8,128)S(1)} all-to-all(f32[128,8,128]{2,1,0:T(8,128)S(1)} %broadcast_in_dim.27), channel_id=1, replica_groups=mesh['src'=32,'sta'=4] {'src','sta'}, dimensions={0} | all-to-all | bytes 1048576 | tf_op jit(solution)/shard_map/all_to_all | solution.py:180
  72.5 1.3 %finish.1 = f32[2,128]{1,0:T(2,128)} custom-call(s32[2]{0:T(128)S(1)} %pad_add_fusion.where, f32[128,8,128]{2,1,0:T(8,128)S(1)} %all_to_all.10.parts), custom_call_target="tpu_custom_call" | custom-call | tf_op jit(solution)/shard_map/finish/pallas_call | solution.py:181
  (12 shorter events, 0.1 us)
Async XLA Ops:
  0.0 0.8 %copy-start.2 = (s32[128,64]{0,1:T(8,128)S(1)}, s32[128,64]{0,1:T(8,128)}, u32[]{:S(2)}) copy-start(s32[128,64]{0,1:T(8,128)} %param.7) | copy-start | bytes 98308
  0.0 1.0 %copy-start = (f32[64,258]{1,0:T(8,128)S(1)}, f32[64,258]{1,0:T(8,128)}, u32[]{:S(2)}) copy-start(f32[64,258]{1,0:T(8,128)} %trace.1) | copy-start | bytes 198148
  1.0 0.9 %copy-start.1 = (f32[64,258]{1,0:T(8,128)S(1)}, f32[64,258]{1,0:T(8,128)}, u32[]{:S(2)}) copy-start(f32[64,258]{1,0:T(8,128)} %quad.1) | copy-start | bytes 198148
  3.6 38.4 %all-to-all-start = ((bf16[128,24,128]{2,1,0:T(8,128)(2,1)}), bf16[128,24,128]{2,1,0:T(8,128)(2,1)S(1)}, u32[]{:S(2)}, u32[]{:S(2)}) async-start(bf16[128,24,128]{2,1,0:T(8,128)(2,1)} %bitcast.3), calls=%async_computation | async-start | bytes 1572864 | tf_op jit(solution)/shard_map/all_to_all | solution.py:156
  14.8 26.4 %collective-permute-start = (f32[64,384]{1,0:T(8,128)S(1)}, f32[64,384]{1,0:T(8,128)S(1)}, u32[]{:S(2)}, u32[]{:S(2)}) collective-permute-start(f32[64,384]{1,0:T(8,128)S(1)} %get-tuple-element.12.e0), channel_id=1, source_target_pairs={{1,0},{2,1},{3,2},{0,3},{5,4},{6,5},{7,6},{4,7},{9,8},{10,9},{11,1... | collective-permute-start | bytes 294920 | tf_op jit(solution)/shard_map/ppermute | solution.py:159
  15.5 25.7 %collective-permute-start.1 = (f32[64,384]{1,0:T(8,128)S(1)}, f32[64,384]{1,0:T(8,128)S(1)}, u32[]{:S(2)}, u32[]{:S(2)}) collective-permute-start(f32[64,384]{1,0:T(8,128)S(1)} %get-tuple-element.12.e0), channel_id=1, source_target_pairs={{2,0},{3,1},{0,2},{1,3},{6,4},{7,5},{4,6},{5,7},{10,8},{11,9},{8,1... | collective-permute-start | bytes 294920 | tf_op jit(solution)/shard_map/ppermute | solution.py:159
  15.9 25.3 %collective-permute-start.2 = (f32[64,384]{1,0:T(8,128)S(1)}, f32[64,384]{1,0:T(8,128)S(1)}, u32[]{:S(2)}, u32[]{:S(2)}) collective-permute-start(f32[64,384]{1,0:T(8,128)S(1)} %get-tuple-element.12.e0), channel_id=1, source_target_pairs={{3,0},{0,1},{1,2},{2,3},{7,4},{4,5},{5,6},{6,7},{11,8},{8,9},{9,10... | collective-permute-start | bytes 294920 | tf_op jit(solution)/shard_map/ppermute | solution.py:159
  16.0 11.3 %collective-permute-start.3 = (f32[64,128]{1,0:T(8,128)S(1)}, f32[64,128]{1,0:T(8,128)S(1)}, u32[]{:S(2)}, u32[]{:S(2)}) collective-permute-start(f32[64,128]{1,0:T(8,128)S(1)} %get-tuple-element.13), channel_id=1, source_target_pairs={{4,0},{8,4},{12,8},{16,12},{20,16},{24,20},{28,24},{32,28},{36,32}... | collective-permute-start | bytes 98312 | tf_op jit(solution)/shard_map/ppermute | solution.py:163
  24.2 11.8 %collective-permute-start.4 = (f32[64,128]{1,0:T(8,128)S(1)}, f32[64,128]{1,0:T(8,128)S(1)}, u32[]{:S(2)}, u32[]{:S(2)}) collective-permute-start(f32[64,128]{1,0:T(8,128)S(1)} %get-tuple-element.14), channel_id=1, source_target_pairs={{0,4},{4,8},{8,12},{12,16},{16,20},{20,24},{24,28},{28,32},{32,36}... | collective-permute-start | bytes 98312 | tf_op jit(solution)/shard_map/ppermute | solution.py:162
  36.0 1.7 %collective-permute-start.5 = (f32[64,128]{1,0:T(8,128)S(1)}, f32[64,128]{1,0:T(8,128)S(1)}, u32[]{:S(2)}, u32[]{:S(2)}) collective-permute-start(f32[64,128]{1,0:T(8,128)S(1)} %broadcast_select_fusion.h0), channel_id=1, source_target_pairs={{1,0},{2,1},{3,2},{0,3},{5,4},{6,5},{7,6},{4,7},{9,8},{10,9},{11,1... | collective-permute-start | bytes 98312 | tf_op jit(solution)/shard_map/ppermute | solution.py:159
  36.0 4.0 %collective-permute-start.6 = (f32[64,128]{1,0:T(8,128)S(1)}, f32[64,128]{1,0:T(8,128)S(1)}, u32[]{:S(2)}, u32[]{:S(2)}) collective-permute-start(f32[64,128]{1,0:T(8,128)S(1)} %broadcast_select_fusion.h0), channel_id=1, source_target_pairs={{2,0},{3,1},{0,2},{1,3},{6,4},{7,5},{4,6},{5,7},{10,8},{11,9},{8,1... | collective-permute-start | bytes 98312 | tf_op jit(solution)/shard_map/ppermute | solution.py:159
  37.7 3.5 %collective-permute-start.7 = (f32[64,128]{1,0:T(8,128)S(1)}, f32[64,128]{1,0:T(8,128)S(1)}, u32[]{:S(2)}, u32[]{:S(2)}) collective-permute-start(f32[64,128]{1,0:T(8,128)S(1)} %broadcast_select_fusion.h0), channel_id=1, source_target_pairs={{3,0},{0,1},{1,2},{2,3},{7,4},{4,5},{5,6},{6,7},{11,8},{8,9},{9,10... | collective-permute-start | bytes 98312 | tf_op jit(solution)/shard_map/ppermute | solution.py:159

commit v2 on v1

--- a/solution.py
+++ b/solution.py
@@ -21,20 +21,34 @@
 BLK = 258
 ST = 64
 STATIONS = ST * STA
-WIN = 256
+HALO = LAGS - 1
+ROWS_OUT = 272
+ROWS_IN = ROWS_OUT + LAGS
 CPD = 128
 ROWS = 24
 SAMPLES = BLK * SRC
 HALF = SRC // STEPS * STA
 
 
-def prologue(where, trace, quad, gains, lags, own, left, right, chunk):
-    tr, qd = trace[...], quad[...]
+def prologue(where, trace, quad, gains, lags, own, near, far, chunk, tr_in, qd_in, ga_in, lg_in, sem):
+    copies = [
+        pltpu.make_async_copy(a, b, sem.at[k])
+        for k, (a, b) in enumerate(((trace, tr_in), (quad, qd_in), (gains, ga_in), (lags, lg_in)))
+    ]
+    for copy in copies:
+        copy.start()
+    for copy in copies:
+        copy.wait()
+    tr, qd = tr_in[...], qd_in[...]
     energy = tr * tr + qd * qd
     own[:, :BLK] = energy
-    own[:, BLK:] = jnp.broadcast_to(gains[...], (ST, 384 - BLK))
-    left[...] = energy[:, BLK - 128 :]
-    right[...] = energy[:, :128]
+    gain = jnp.concatenate([ga_in[...], ga_in[...]], axis=1)
+    gain = jnp.broadcast_to(gain, (128, 128)).T[:ST]
+    own[:, BLK:] = gain[:, : 384 - BLK]
+    first, last = energy[:, :128], energy[:, BLK - 128 :]
+    low_half = where[0] < SRC // STEPS
+    near[...] = jnp.where(low_half, first, last)
+    far[...] = jnp.where(low_half, last, first)
     total = jnp.sum(energy, axis=1, keepdims=True)
     total = jnp.broadcast_to(total, (ST, 128))
     total = jnp.concatenate([total, total], axis=0).T[:8]
@@ -45,10 +59,10 @@
     lane = lax.broadcasted_iota(jnp.int32, (8, 128), 1)
     sums = jnp.where(row == 0, hi, jnp.where(row == 1, mid, jnp.where(row == 2, low, 0.0)))
     sums = jnp.where(lane // ST == where[1] % 2, sums, 0.0)
+    lag = lg_in[...].astype(F32)
+    lag = jnp.concatenate([lag, lag], axis=0).T
     for j in range(STA):
-        first = lags[32 * j : 32 * j + 16, :]
-        second = lags[32 * j + 16 : 32 * j + 32, :]
-        body = jnp.concatenate([first, second], axis=1).astype(F32)
+        body = jnp.where(lane[:1] < ST, lag[32 * j : 32 * j + 16], lag[32 * j + 16 : 32 * j + 32])
         chunk[j] = jnp.concatenate([body, sums], axis=0).astype(BF16)
 
 
@@ -59,14 +73,16 @@
         edges[pl.ds(at, ST), :] = h[...]
     side = edges[...].T
     main = tall[...].T
-    line[64:448, :] = main
-    line[0:64, :] = side[64:128]
-    line[64 + BLK : 64 + BLK + 64, :] = side[0:64]
-    win[...] = pltpu.roll(line[...], 448 - 64 + 2 * where[0], 0)[:320]
+    line[0:128, :] = side
+    line[128:512, :] = main
+    line[128 + BLK : 128 + BLK + 64, :] = side[0:64]
+    ahead = line[128 : 128 + ROWS_IN, :]
+    behind = line[128 - HALO : 128 - HALO + ROWS_IN, :]
+    win[...] = jnp.where(where[0] < SRC // STEPS, ahead, behind)
     gains[...] = jnp.broadcast_to(main[BLK : BLK + 1], (8, STATIONS))
 
 
-def beams(received, win, gains, power, weighted, lagged):
+def beams(where, received, win, gains, power, weighted, lagged):
     halves = []
     for half in range(2):
         acc = jnp.zeros((8, 128), F32)
@@ -77,8 +93,12 @@
     baseline = jnp.concatenate(halves, axis=1) / SAMPLES
     gain = gains[0:1, :]
     for b in range(16):
-        rows = 304 if b < 15 else 304
-        weighted[b] = (gain * (win[b : b + rows, :] - baseline)).astype(BF16)
+        weighted[b] = (gain * (win[b : b + ROWS_OUT + 48, :] - baseline)).astype(BF16)
+    src = where[0]
+    start = jnp.where(src == SRC // STEPS, W - (BLK * (SRC // STEPS) - HALO), 0)
+    stop = jnp.where(src == SRC // STEPS - 1, W - BLK * (SRC // STEPS - 1), jnp.where(src == SRC - 1, BLK - 1, BLK))
+    row = lax.broadcasted_iota(jnp.int32, (ROWS_OUT, 256), 0)
+    inside = jnp.logical_and(row >= start, row < stop)
     for j in range(STA):
         part = jnp.concatenate([received[STA * i + j, 0:16, :] for i in range(SRC)], axis=0)
         part = part.astype(F32).T.astype(BF16)
@@ -94,12 +114,13 @@
             for b in range(16):
                 value = (base + b).astype(F32).astype(BF16)
                 picks.append(jnp.where(lag == value, BF16(1), BF16(0)))
-                shifted.append(weighted[b, pl.ds(base, WIN), :])
+                shifted.append(weighted[b, pl.ds(base, ROWS_OUT), :])
             return total + jnp.dot(
                 jnp.concatenate(shifted, axis=1), jnp.concatenate(picks, axis=0), preferred_element_type=F32
             )
 
-        beam = lax.fori_loop(0, LAGS // 16, add, jnp.zeros((WIN, 256), F32))
+        beam = lax.fori_loop(0, LAGS // 16, add, jnp.zeros((ROWS_OUT, 256), F32))
+        beam = jnp.where(inside, beam, 0.0)
         squared = jnp.sum(beam * beam, axis=0, keepdims=True)
         power[2 * group : 2 * group + 1, :] = squared[:, :128]
         power[2 * group + 1 : 2 * group + 2, :] = squared[:, 128:]
@@ -146,37 +167,45 @@
 
 def on_device(trace, quadrature, gains, lags):
     where = jnp.stack([lax.axis_index("src"), lax.axis_index("sta")]).astype(jnp.int32)
-    own, left, right, chunk = call(
+    own, near, far, chunk = call(
         prologue,
         [shape((ST, 384)), shape((ST, 128)), shape((ST, 128)), shape((STA, ROWS, 128), BF16)],
-        [SMEM] + [VMEM] * 4,
+        [SMEM] + [pl.BlockSpec(memory_space=pl.ANY)] * 4,
+        [
+            pltpu.VMEM((ST, BLK), F32),
+            pltpu.VMEM((ST, BLK), F32),
+            pltpu.VMEM((1, ST), F32),
+            pltpu.VMEM((ST, CPD), jnp.int32),
+            pltpu.SemaphoreType.DMA((4,)),
+        ],
         name="prologue",
-    )(where, trace, quadrature, gains[:, None], lags)
+    )(where, trace, quadrature, gains[None], lags.T)
     chunks = jnp.broadcast_to(chunk[None], (SRC, STA, ROWS, 128)).reshape(DEV, ROWS, 128)
     received = lax.all_to_all(chunks, ("src", "sta"), 0, 0, tiled=True)
 
     def from_sta(x, k):
         return lax.ppermute(x, "sta", [((j + k) % STA, j) for j in range(STA)])
 
+    middle = SRC // STEPS
+    pairs = [(i + 1, i) for i in range(middle - 1)] + [(i - 1, i) for i in range(middle + 1, SRC)]
+    edge = lax.ppermute(near, "src", pairs)
+    edge = edge + lax.ppermute(far, "src", [(middle, middle - 1), (middle - 1, middle)])
     blocks = [own] + [from_sta(own, k) for k in range(1, STA)]
-    before = lax.ppermute(left, "src", [(i, (i + 1) % SRC) for i in range(SRC)])
-    after = lax.ppermute(right, "src", [((i + 1) % SRC, i) for i in range(SRC)])
-    edge = jnp.where(jnp.arange(128)[None, :] < 64, after, before)
     edges = [edge] + [from_sta(edge, k) for k in range(1, STA)]
     win, gain = call(
         window,
-        [shape((320, STATIONS)), shape((8, STATIONS))],
+        [shape((ROWS_IN, STATIONS)), shape((8, STATIONS))],
         [SMEM] + [VMEM] * 8,
-        [pltpu.VMEM((STATIONS, 384), F32), pltpu.VMEM((STATIONS, 128), F32), pltpu.VMEM((448, STATIONS), F32)],
+        [pltpu.VMEM((STATIONS, 384), F32), pltpu.VMEM((STATIONS, 128), F32), pltpu.VMEM((512, STATIONS), F32)],
         name="window",
     )(where, *blocks, *edges)
     power = call(
         beams,
         shape((8, 128)),
-        [VMEM] * 3,
-        [pltpu.VMEM((16, 304, STATIONS), BF16), pltpu.VMEM((2, STATIONS, 512), BF16)],
+        [SMEM] + [VMEM] * 3,
+        [pltpu.VMEM((16, ROWS_OUT + 48, STATIONS), BF16), pltpu.VMEM((2, STATIONS, 512), BF16)],
         name="beams",
-    )(received, win, gain)
+    )(where, received, win, gain)
     parts = lax.all_to_all(jnp.broadcast_to(power[None], (DEV, 8, 128)), ("src", "sta"), 0, 0, tiled=True)
     return call(finish, shape((STEPS, CPD)), [SMEM, VMEM], [pltpu.VMEM((32, 128), F32)], name="finish")(where, parts)
 

time: 74.7 us -> 74.4 us (level)
  waiting for transfers between devices: 15.2 us -> 8.62 us
  blocking collectives: 17.5 us -> 23.1 us
  starting transfers between devices: 22.4 us -> 19.8 us
  Pallas kernels: 15.7 us -> 17.4 us
  local copies, waits for them, and re-layouts: 2.83 us -> 4.24 us
    ppermute x2, waiting for transfers between devices: 11.8 us -> 5.37 us  [the longest x1 5.37 us: on_device(): edge = lax.ppermute(near, 'src', pairs)]
    ppermute x2, starting transfers between devices: 8.15 us -> 1.96 us  [the longest x1 1.29 us: on_device(): edge = lax.ppermute(near, 'src', pairs)]
    all_to_all x1, blocking collectives: 17.5 us -> 23.1 us  [on_device(): lax.all_to_all(jnp.broadcast_to(power[None], (DEV, 8, 128)), ('src', 'sta...]
    ppermute x6, starting transfers between devices: 3.05 us -> 6.7 us  [from_sta(): return lax.ppermute(x, 'sta', [((j + k) % STA, j) for j in range(STA)])]
    unnamed x7 -> x8, local copies, waits for them, and re-layouts: 0.99 us -> 3.2 us
    pallas_call x2, Pallas kernels: 13.7 us -> 14.9 us  [the longest x1 14.1 us: on_device(): call(beams, shape((8, 128)), [SMEM] + [VMEM] * 3, [pltpu.VMEM((16, ROWS_O...]
    broadcast_in_dim x1 -> x0, local copies, waits for them, and re-layouts: 0.78 us -> none  [on_device(): gains[:, None]]
  transfers between devices with their start and end apart: 9 -> 9, of which waited for: 5 -> 4; matrix products, arithmetic and copies ran while one was open for 0% -> 0% of each run, Pallas kernels for 1% -> 1%
where the time goes in v2:
time: 74.4 us; the launch traced here: 73.4 us
  blocking collectives  23.1 us (31%)
  starting transfers between devices  19.8 us (27%)
  Pallas kernels  17.4 us (23%)
  waiting for transfers between devices  8.62 us (12%)
  local copies, waits for them, and re-layouts  4.24 us (6%)
    all_to_all x1, blocking collectives, on_device(): lax.all_to_all(jnp.broadcast_to(power[None], (DEV, 8, 128)), ('src', 'sta...  23.1 us
    pallas_call x1, Pallas kernels, on_device(): call(beams, shape((8, 128)), [SMEM] + [VMEM] * 3, [pltpu.VMEM((16, ROWS_O...  14.1 us
    all_to_all x1, starting transfers between devices, on_device(): received = lax.all_to_all(chunks, ('src', 'sta'), 0, 0, tiled=True)  11.2 us
    ppermute x6, starting transfers between devices, from_sta(): return lax.ppermute(x, 'sta', [((j + k) % STA, j) for j in range(STA)])  6.7 us
    ppermute x1, waiting for transfers between devices, on_device(): edge = lax.ppermute(near, 'src', pairs)  5.37 us
    ppermute x6, waiting for transfers between devices, from_sta(): return lax.ppermute(x, 'sta', [((j + k) % STA, j) for j in range(STA)])  3.25 us
    unnamed x8, local copies, waits for them, and re-layouts  3.2 us
  transfers between devices with their start and end apart: 9, of which 4 were waited for; matrix products, arithmetic and copies ran while one was open for 0% of the time, Pallas kernels for 1%

profile of v2, /device:TPU:0, one launch (start us, length us, event | category | flops | bytes accessed | tf_op | source)
XLA Modules:
  0.0 73.4 jit_solution(4059561701755161282)
XLA Ops:
  0.0 0.1 pad_add_fusion.where
  0.1 0.7 copy-done.3
  0.7 0.9 %copy-done = f32[64,258]{1,0:T(8,128)S(1)} copy-done((f32[64,258]{1,0:T(8,128)S(1)}, f32[64,258]{1,0:T(8,128)}, u32[]{:S(2)}) %copy-start) | copy-done | bytes 66072
  1.6 0.9 %copy-done.1 = f32[64,258]{1,0:T(8,128)S(1)} copy-done((f32[64,258]{1,0:T(8,128)S(1)}, f32[64,258]{1,0:T(8,128)}, u32[]{:S(2)}) %copy-start.1) | copy-done | bytes 66072
  2.5 0.8 %copy-done.2 = s32[128,64]{0,1:T(8,128)S(1)} copy-done((s32[128,64]{0,1:T(8,128)S(1)}, s32[128,64]{0,1:T(8,128)}, u32[]{:S(2)}) %copy-start.2) | copy-done | bytes 32792
  3.3 1.2 %prologue.1 = (f32[64,384]{1,0:T(8,128)S(1)}, f32[64,128]{1,0:T(8,128)S(1)}, f32[64,128]{1,0:T(8,128)S(1)}, bf16[4,24,128]{2,1,0:T(8,128)(2,1)S(1)}) custom-call(s32[2]{0:T(128)S(1)} %pad_add_fusion.where, f32[64,258]{1,0:T(8,128)S(1)} %copy-done, f32[64,258]{1,0:T(8,128)S(1)} %copy-done.1, f32[1,64]{1,0:T(1,128)S(1)} %bitcast.6, s32[64,128]{1,0:T(8,128)S(1)} %bitcast.5), custom_call_target="tpu_custom_call" | custom-call | tf_op jit(solution)/shard_map/prologue/pallas_call | solution.py:170
  4.5 1.0 %broadcast_in_dim.7 = bf16[32,4,24,128]{3,2,1,0:T(8,128)(2,1)} broadcast(bf16[4,24,128]{2,1,0:T(8,128)(2,1)S(1)} %get-tuple-element.11), dimensions={1,2,3} | broadcast | bytes 811008 | tf_op jit(solution)/shard_map/broadcast_in_dim | solution.py:183
  5.5 11.2 %all-to-all-start = ((bf16[128,24,128]{2,1,0:T(8,128)(2,1)}), bf16[128,24,128]{2,1,0:T(8,128)(2,1)S(1)}, u32[]{:S(2)}, u32[]{:S(2)}) async-start(bf16[128,24,128]{2,1,0:T(8,128)(2,1)} %bitcast.4), calls=%async_computation | async-start | bytes 1572864 | tf_op jit(solution)/shard_map/all_to_all | solution.py:184
  16.7 1.3 %collective-permute-start.3 = (f32[64,128]{1,0:T(8,128)S(1)}, f32[64,128]{1,0:T(8,128)S(1)}, u32[]{:S(2)}, u32[]{:S(2)}) collective-permute-start(f32[64,128]{1,0:T(8,128)S(1)} %get-tuple-element.13), channel_id=1, source_target_pairs={{4,0},{8,4},{12,8},{16,12},{20,16},{24,20},{28,24},{32,28},{36,32}... | collective-permute-start | bytes 98312 | tf_op jit(solution)/shard_map/ppermute | solution.py:191
  18.0 0.7 collective-permute-start.4
  18.7 0.7 %collective-permute-start = (f32[64,384]{1,0:T(8,128)S(1)}, f32[64,384]{1,0:T(8,128)S(1)}, u32[]{:S(2)}, u32[]{:S(2)}) collective-permute-start(f32[64,384]{1,0:T(8,128)S(1)} %get-tuple-element.12.e0), channel_id=1, source_target_pairs={{1,0},{2,1},{3,2},{0,3},{5,4},{6,5},{7,6},{4,7},{9,8},{10,9},{11,1... | collective-permute-start | bytes 294920 | tf_op jit(solution)/shard_map/ppermute | solution.py:187
  19.4 0.4 collective-permute-start.1
  19.8 0.1 collective-permute-start.2
  19.9 5.4 %collective-permute-done.3 = f32[64,128]{1,0:T(8,128)S(1)} collective-permute-done((f32[64,128]{1,0:T(8,128)S(1)}, f32[64,128]{1,0:T(8,128)S(1)}, u32[]{:S(2)}, u32[]{:S(2)}) %collective-permute-start.3) | collective-permute-done | bytes 32800 | tf_op jit(solution)/shard_map/ppermute | solution.py:191
  25.3 3.4 %collective-permute-start.5 = (f32[64,128]{1,0:T(8,128)S(1)}, f32[64,128]{1,0:T(8,128)S(1)}, u32[]{:S(2)}, u32[]{:S(2)}) collective-permute-start(f32[64,128]{1,0:T(8,128)S(1)} %add.3.h0), channel_id=1, source_target_pairs={{1,0},{2,1},{3,2},{0,3},{5,4},{6,5},{7,6},{4,7},{9,8},{10,9},{11,1... | collective-permute-start | bytes 98312 | tf_op jit(solution)/shard_map/ppermute | solution.py:187
  28.7 0.8 %collective-permute-start.6 = (f32[64,128]{1,0:T(8,128)S(1)}, f32[64,128]{1,0:T(8,128)S(1)}, u32[]{:S(2)}, u32[]{:S(2)}) collective-permute-start(f32[64,128]{1,0:T(8,128)S(1)} %add.3.h0), channel_id=1, source_target_pairs={{2,0},{3,1},{0,2},{1,3},{6,4},{7,5},{4,6},{5,7},{10,8},{11,9},{8,1... | collective-permute-start | bytes 98312 | tf_op jit(solution)/shard_map/ppermute | solution.py:187
  29.5 0.8 %collective-permute-done.5.h1 = f32[64,128]{1,0:T(8,128)S(1)} collective-permute-done((f32[64,128]{1,0:T(8,128)S(1)}, f32[64,128]{1,0:T(8,128)S(1)}, u32[]{:S(2)}, u32[]{:S(2)}) %collective-permute-start.5) | collective-permute-done | bytes 32800 | tf_op jit(solution)/shard_map/ppermute | solution.py:187
  30.3 1.3 %collective-permute-start.7 = (f32[64,128]{1,0:T(8,128)S(1)}, f32[64,128]{1,0:T(8,128)S(1)}, u32[]{:S(2)}, u32[]{:S(2)}) collective-permute-start(f32[64,128]{1,0:T(8,128)S(1)} %add.3.h0), channel_id=1, source_target_pairs={{3,0},{0,1},{1,2},{2,3},{7,4},{4,5},{5,6},{6,7},{11,8},{8,9},{9,10... | collective-permute-start | bytes 98312 | tf_op jit(solution)/shard_map/ppermute | solution.py:187
  31.6 1.0 %collective-permute-done.6.h2 = f32[64,128]{1,0:T(8,128)S(1)} collective-permute-done((f32[64,128]{1,0:T(8,128)S(1)}, f32[64,128]{1,0:T(8,128)S(1)}, u32[]{:S(2)}, u32[]{:S(2)}) %collective-permute-start.6) | collective-permute-done | bytes 32800 | tf_op jit(solution)/shard_map/ppermute | solution.py:187
  32.6 1.4 %collective-permute-done.7.h3 = f32[64,128]{1,0:T(8,128)S(1)} collective-permute-done((f32[64,128]{1,0:T(8,128)S(1)}, f32[64,128]{1,0:T(8,128)S(1)}, u32[]{:S(2)}, u32[]{:S(2)}) %collective-permute-start.7) | collective-permute-done | bytes 32800 | tf_op jit(solution)/shard_map/ppermute | solution.py:187
  34.0 0.8 %window.1 = (f32[336,256]{1,0:T(8,128)S(1)}, f32[8,256]{1,0:T(8,128)S(1)}) custom-call(s32[2]{0:T(128)S(1)} %pad_add_fusion.where, f32[64,384]{1,0:T(8,128)S(1)} %get-tuple-element.12.e0, f32[64,384]{1,0:T(8,128)S(1)} %collective-permute-done.e1, f32[64,384]{1,0:T(8,128)S(1)} %collective-permute-done.1.e2, f32[64,384]{1,0:T(8,128)S(1)} %collective-permute-done.2.e3, ...), custom_call_target="tpu_custom_call" | custom-call | tf_op jit(solution)/shard_map/window/pallas_call | solution.py:195
  34.8 14.1 %beams.1 = f32[8,128]{1,0:T(8,128)S(1)} custom-call(s32[2]{0:T(128)S(1)} %pad_add_fusion.where, bf16[128,24,128]{2,1,0:T(8,128)(2,1)S(1)} %all-to-all-done.received, f32[336,256]{1,0:T(8,128)S(1)} %get-tuple-element.15.win, f32[8,256]{1,0:T(8,128)S(1)} %get-tuple-element.16.gains), custom_call_target="tpu_custom_call" | custom-call | tf_op jit(solution)/shard_map/beams/pallas_call | solution.py:202
  49.0 23.1 %all_to_all.10.parts = f32[128,8,128]{2,1,0:T(8,128)S(1)} all-to-all(f32[128,8,128]{2,1,0:T(8,128)S(1)} %broadcast_in_dim.8), channel_id=1, replica_groups=mesh['src'=32,'sta'=4] {'src','sta'}, dimensions={0} | all-to-all | bytes 1048576 | tf_op jit(solution)/shard_map/all_to_all | solution.py:209
  72.1 1.3 %finish.1 = f32[2,128]{1,0:T(2,128)} custom-call(s32[2]{0:T(128)S(1)} %pad_add_fusion.where, f32[128,8,128]{2,1,0:T(8,128)S(1)} %all_to_all.10.parts), custom_call_target="tpu_custom_call" | custom-call | tf_op jit(solution)/shard_map/finish/pallas_call | solution.py:210
  (11 shorter events, 0.1 us)
Async XLA Ops:
  0.1 0.7 copy-start.3
  0.7 0.9 %copy-start = (f32[64,258]{1,0:T(8,128)S(1)}, f32[64,258]{1,0:T(8,128)}, u32[]{:S(2)}) copy-start(f32[64,258]{1,0:T(8,128)} %trace.1) | copy-start | bytes 198148
  1.6 0.9 %copy-start.1 = (f32[64,258]{1,0:T(8,128)S(1)}, f32[64,258]{1,0:T(8,128)}, u32[]{:S(2)}) copy-start(f32[64,258]{1,0:T(8,128)} %quad.1) | copy-start | bytes 198148
  2.5 0.8 %copy-start.2 = (s32[128,64]{0,1:T(8,128)S(1)}, s32[128,64]{0,1:T(8,128)}, u32[]{:S(2)}) copy-start(s32[128,64]{0,1:T(8,128)} %param.7) | copy-start | bytes 98308
  5.5 29.3 %all-to-all-start = ((bf16[128,24,128]{2,1,0:T(8,128)(2,1)}), bf16[128,24,128]{2,1,0:T(8,128)(2,1)S(1)}, u32[]{:S(2)}, u32[]{:S(2)}) async-start(bf16[128,24,128]{2,1,0:T(8,128)(2,1)} %bitcast.4), calls=%async_computation | async-start | bytes 1572864 | tf_op jit(solution)/shard_map/all_to_all | solution.py:184
  16.7 8.6 %collective-permute-start.3 = (f32[64,128]{1,0:T(8,128)S(1)}, f32[64,128]{1,0:T(8,128)S(1)}, u32[]{:S(2)}, u32[]{:S(2)}) collective-permute-start(f32[64,128]{1,0:T(8,128)S(1)} %get-tuple-element.13), channel_id=1, source_target_pairs={{4,0},{8,4},{12,8},{16,12},{20,16},{24,20},{28,24},{32,28},{36,32}... | collective-permute-start | bytes 98312 | tf_op jit(solution)/shard_map/ppermute | solution.py:191
  18.0 7.3 %collective-permute-start.4 = (f32[64,128]{1,0:T(8,128)S(1)}, f32[64,128]{1,0:T(8,128)S(1)}, u32[]{:S(2)}, u32[]{:S(2)}) collective-permute-start(f32[64,128]{1,0:T(8,128)S(1)} %get-tuple-element.14), channel_id=1, source_target_pairs={{64,60},{60,64},{65,61},{61,65},{66,62},{62,66},{67,63},{63,67}} | collective-permute-start | bytes 98312 | tf_op jit(solution)/shard_map/ppermute | solution.py:192
  18.7 15.3 %collective-permute-start = (f32[64,384]{1,0:T(8,128)S(1)}, f32[64,384]{1,0:T(8,128)S(1)}, u32[]{:S(2)}, u32[]{:S(2)}) collective-permute-start(f32[64,384]{1,0:T(8,128)S(1)} %get-tuple-element.12.e0), channel_id=1, source_target_pairs={{1,0},{2,1},{3,2},{0,3},{5,4},{6,5},{7,6},{4,7},{9,8},{10,9},{11,1... | collective-permute-start | bytes 294920 | tf_op jit(solution)/shard_map/ppermute | solution.py:187
  19.4 14.6 %collective-permute-start.1 = (f32[64,384]{1,0:T(8,128)S(1)}, f32[64,384]{1,0:T(8,128)S(1)}, u32[]{:S(2)}, u32[]{:S(2)}) collective-permute-start(f32[64,384]{1,0:T(8,128)S(1)} %get-tuple-element.12.e0), channel_id=1, source_target_pairs={{2,0},{3,1},{0,2},{1,3},{6,4},{7,5},{4,6},{5,7},{10,8},{11,9},{8,1... | collective-permute-start | bytes 294920 | tf_op jit(solution)/shard_map/ppermute | solution.py:187
  19.8 14.2 %collective-permute-start.2 = (f32[64,384]{1,0:T(8,128)S(1)}, f32[64,384]{1,0:T(8,128)S(1)}, u32[]{:S(2)}, u32[]{:S(2)}) collective-permute-start(f32[64,384]{1,0:T(8,128)S(1)} %get-tuple-element.12.e0), channel_id=1, source_target_pairs={{3,0},{0,1},{1,2},{2,3},{7,4},{4,5},{5,6},{6,7},{11,8},{8,9},{9,10... | collective-permute-start | bytes 294920 | tf_op jit(solution)/shard_map/ppermute | solution.py:187
  25.3 5.0 %collective-permute-start.5 = (f32[64,128]{1,0:T(8,128)S(1)}, f32[64,128]{1,0:T(8,128)S(1)}, u32[]{:S(2)}, u32[]{:S(2)}) collective-permute-start(f32[64,128]{1,0:T(8,128)S(1)} %add.3.h0), channel_id=1, source_target_pairs={{1,0},{2,1},{3,2},{0,3},{5,4},{6,5},{7,6},{4,7},{9,8},{10,9},{11,1... | collective-permute-start | bytes 98312 | tf_op jit(solution)/shard_map/ppermute | solution.py:187
  28.7 3.9 %collective-permute-start.6 = (f32[64,128]{1,0:T(8,128)S(1)}, f32[64,128]{1,0:T(8,128)S(1)}, u32[]{:S(2)}, u32[]{:S(2)}) collective-permute-start(f32[64,128]{1,0:T(8,128)S(1)} %add.3.h0), channel_id=1, source_target_pairs={{2,0},{3,1},{0,2},{1,3},{6,4},{7,5},{4,6},{5,7},{10,8},{11,9},{8,1... | collective-permute-start | bytes 98312 | tf_op jit(solution)/shard_map/ppermute | solution.py:187
  30.3 3.7 %collective-permute-start.7 = (f32[64,128]{1,0:T(8,128)S(1)}, f32[64,128]{1,0:T(8,128)S(1)}, u32[]{:S(2)}, u32[]{:S(2)}) collective-permute-start(f32[64,128]{1,0:T(8,128)S(1)} %add.3.h0), channel_id=1, source_target_pairs={{3,0},{0,1},{1,2},{2,3},{7,4},{4,5},{5,6},{6,7},{11,8},{8,9},{9,10... | collective-permute-start | bytes 98312 | tf_op jit(solution)/shard_map/ppermute | solution.py:187

commit v3 on v2

v3 whole, which is shorter than its diff:
```python
import jax
import jax.numpy as jnp
from jax import lax
from jax.experimental import pallas as pl
from jax.experimental.pallas import tpu as pltpu
from jax.sharding import PartitionSpec as P


W = 4096
LAGS = 64
STEPS = 2
F32 = jnp.float32
BF16 = jnp.bfloat16
VMEM = pl.BlockSpec(memory_space=pltpu.VMEM)
SMEM = pl.BlockSpec(memory_space=pltpu.SMEM)

SRC = 32
STA = 4
DEV = SRC * STA
BLK = 258
ST = 64
STATIONS = ST * STA
HALO = LAGS - 1
CHAIN = 64
ROWS_OUT = 264
ROWS_IN = ROWS_OUT + LAGS
CPD = 128
ROWS = 24
SAMPLES = BLK * SRC
HALF = SRC // STEPS * STA


def prologue(where, trace, quad, gains, lags, own, chunk, tr_in, qd_in, ga_in, lg_in, sem):
    copies = [
        pltpu.make_async_copy(a, b, sem.at[k])
        for k, (a, b) in enumerate(((trace, tr_in), (quad, qd_in), (gains, ga_in), (lags, lg_in)))
    ]
    for copy in copies:
        copy.start()
    for copy in copies:
        copy.wait()
    tr, qd = tr_in[...], qd_in[...]
    energy = tr * tr + qd * qd
    own[:, :BLK] = energy
    gain = jnp.concatenate([ga_in[...], ga_in[...]], axis=1)
    gain = jnp.broadcast_to(gain, (128, 128)).T[:ST]
    own[:, BLK:] = gain[:, : 384 - BLK]
    total = jnp.sum(energy, axis=1, keepdims=True)
    total = jnp.broadcast_to(total, (ST, 128))
    total = jnp.concatenate([total, total], axis=0).T[:8]
    hi = total.astype(BF16).astype(F32)
    mid = (total - hi).astype(BF16).astype(F32)
    low = total - hi - mid
    row = lax.broadcasted_iota(jnp.int32, (8, 128), 0)
    lane = lax.broadcasted_iota(jnp.int32, (8, 128), 1)
    sums = jnp.where(row == 0, hi, jnp.where(row == 1, mid, jnp.where(row == 2, low, 0.0)))
    sums = jnp.where(lane // ST == where[1] % 2, sums, 0.0)
    lag = lg_in[...].astype(F32)
    lag = jnp.concatenate([lag, lag], axis=0).T
    for j in range(STA):
        body = jnp.where(lane[:1] < ST, lag[32 * j : 32 * j + 16], lag[32 * j + 16 : 32 * j + 32])
        chunk[j] = jnp.concatenate([body, sums], axis=0).astype(BF16)


def turn(where, e0, e1, e2, e3, main, near, far, tall):
    for k, e in enumerate((e0, e1, e2, e3)):
        at = pl.multiple_of((where[1] + k) % STA * ST, ST)
        tall[pl.ds(at, ST), :] = e[...]
    main[...] = tall[...].T
    first, last = main[0:64, :], main[BLK - 64 : BLK, :]
    low_half = where[0] < SRC // STEPS
    near[...] = jnp.where(low_half, first, last)
    far[...] = jnp.where(low_half, last, first)


def beams(where, received, main, halo, far_halo, power, line, weighted, lagged):
    halves = []
    for half in range(2):
        acc = jnp.zeros((8, 128), F32)
        for i in range(SRC):
            for j in (2 * half, 2 * half + 1):
                acc = acc + received[STA * i + j, 16:24, :].astype(F32)
        halves.append(jnp.sum(acc, axis=0, keepdims=True))
    baseline = jnp.concatenate(halves, axis=1) / SAMPLES
    gain = main[BLK : BLK + 1, :]

    def weigh(energy):
        return (gain * (energy - baseline)).astype(BF16).astype(F32)

    src = where[0]
    middle = SRC // STEPS
    edge = weigh(halo[...] + far_halo[...])

    @pl.when(src < middle)
    def _():
        line[0:264, :] = weigh(main[0:264, :])
        line[BLK : BLK + 64, :] = edge

    @pl.when(src >= middle)
    def _():
        line[0:HALO, :] = edge[1:64]
        line[HALO : HALO + 264, :] = weigh(main[0:264, :])

    for b in range(16):
        weighted[b] = line[b : b + ROWS_OUT + 48, :].astype(BF16)
    start = jnp.where(src == middle, W - (BLK * middle - HALO), 0)
    stop = jnp.where(src == middle - 1, W - BLK * (middle - 1), jnp.where(src == SRC - 1, BLK - 1, BLK))
    row = lax.broadcasted_iota(jnp.int32, (ROWS_OUT, 256), 0)
    inside = jnp.logical_and(row >= start, row < stop)
    for j in range(STA):
        part = jnp.concatenate([received[STA * i + j, 0:16, :] for i in range(SRC)], axis=0)
        part = part.astype(F32).T.astype(BF16)
        for group in range(4):
            lagged[group, ST * j : ST * j + ST, :] = part[
                ST * (group // 2) : ST * (group // 2) + ST, 256 * (group % 2) : 256 * (group % 2) + 256
            ]

    def one(group, carry):
        lag = lagged[group]

        def add(step, total):
            base = pl.multiple_of(step * CHAIN, 16)
            picks, shifted = [], []
            for b in range(CHAIN):
                value = (base + b).astype(F32).astype(BF16) if CHAIN < LAGS else BF16(b)
                picks.append(jnp.where(lag == value, BF16(1), BF16(0)))
                shifted.append(weighted[b % 16, pl.ds(base + b // 16 * 16, ROWS_OUT), :])
            return total + jnp.dot(
                jnp.concatenate(shifted, axis=1), jnp.concatenate(picks, axis=0), preferred_element_type=F32
            )

        if CHAIN < LAGS:
            beam = lax.fori_loop(0, LAGS // CHAIN, add, jnp.zeros((ROWS_OUT, 256), F32))
        else:
            beam = add(0, 0.0)
        beam = jnp.where(inside, beam, 0.0)
        squared = jnp.sum(beam * beam, axis=0, keepdims=True)
        power[group, 0] = squared[:, :128]
        power[group, 1] = squared[:, 128:]
        return carry

    lax.fori_loop(0, 4, one, 0)


def finish(where, parts, out, sums):
    src = where[0]
    lane = lax.broadcasted_iota(jnp.int32, (1, 128), 1)
    for k in range(STEPS):
        peak = None
        for j in range(STA):
            acc = parts[k * HALF + j]
            for i in range(1, SRC // STEPS):
                acc = acc + parts[k * HALF + STA * i + j]
            sums[8 * j : 8 * j + 8, :] = acc
            peak = acc if peak is None else jnp.maximum(peak, acc)
        peak = jnp.max(peak, axis=(0, 1), keepdims=True)
        cells = jnp.zeros((1, 128), F32)
        for j in range(STA):
            for h in range(2):
                row = sums[pl.ds(8 * j + 4 * h + src // 8, 1), :]
                to = 32 * j + 16 * h
                row = pltpu.roll(row, (to - 16 * (src % 8)) % 128, 1)
                cells = jnp.where(lane // 16 == to // 16, row, cells)
        out[k : k + 1, :] = cells / peak


def call(kernel, out_shape, specs, scratch=()):
    multi = isinstance(out_shape, (list, tuple))
    return pl.pallas_call(
        kernel,
        out_shape=out_shape,
        in_specs=specs,
        out_specs=[VMEM] * len(out_shape) if multi else VMEM,
        scratch_shapes=scratch,
        compiler_params=pltpu.CompilerParams(vmem_limit_bytes=48 << 20),
    )


def shape(dims, dtype=F32):
    return jax.ShapeDtypeStruct(dims, dtype)


def program(trace, quadrature, gains, lags):
    where = jnp.stack([lax.axis_index("src"), lax.axis_index("sta")]).astype(jnp.int32)
    inputs = [pltpu.with_memory_space_constraint(x, pltpu.HBM) for x in (trace, quadrature, gains[None], lags.T)]
    own, chunk = call(
        prologue,
        [shape((ST, 384)), shape((STA, ROWS, 128), BF16)],
        [SMEM] + [pl.BlockSpec(memory_space=pltpu.HBM)] * 4,
        [
            pltpu.VMEM((ST, BLK), F32),
            pltpu.VMEM((ST, BLK), F32),
            pltpu.VMEM((1, ST), F32),
            pltpu.VMEM((ST, CPD), jnp.int32),
            pltpu.SemaphoreType.DMA((4,)),
        ],
    )(where, *inputs)
    blocks = [own]
    for k in range(1, STA):
        blocks.append(lax.ppermute(own, "sta", [((j + k) % STA, j) for j in range(STA)]))
    chunks = jnp.broadcast_to(chunk[None], (SRC, STA, ROWS, 128)).reshape(DEV, ROWS, 128)
    received = lax.all_to_all(chunks, ("src", "sta"), 0, 0, tiled=True)
    main, near, far = call(
        turn,
        [shape((384, STATIONS)), shape((64, STATIONS)), shape((64, STATIONS))],
        [SMEM] + [VMEM] * 4,
        [pltpu.VMEM((STATIONS, 384), F32)],
    )(where, *blocks)
    middle = SRC // STEPS
    pairs = [(i + 1, i) for i in range(middle - 1)] + [(i - 1, i) for i in range(middle + 1, SRC)]
    halo = lax.ppermute(near, "src", pairs)
    far_halo = lax.ppermute(far, "src", [(middle, middle - 1), (middle - 1, middle)])
    power = call(
        beams,
        shape((4, 2, 1, 128)),
        [SMEM] + [VMEM] * 4,
        [
            pltpu.VMEM((ROWS_IN, STATIONS), F32),
            pltpu.VMEM((16, ROWS_OUT + 48, STATIONS), BF16),
            pltpu.VMEM((4, STATIONS, 256), BF16),
        ],
    )(where, received, main, halo, far_halo)
    power = power.reshape(8, 128)
    parts = lax.all_to_all(jnp.broadcast_to(power[None], (DEV, 8, 128)), ("src", "sta"), 0, 0, tiled=True)
    return call(finish, shape((STEPS, CPD)), [SMEM, VMEM], [pltpu.VMEM((32, 128), F32)])(where, parts)


def solution(mesh):
    return jax.shard_map(
        program,
        mesh=mesh,
        in_specs=(P("sta", "src"), P("sta", "src"), P("sta"), P("src", "sta")),
        out_specs=P(None, "src"),
        check_vma=False,
    )
```

time: 74.4 us -> 77.1 us (1.036)
  waiting for transfers between devices: 8.62 us -> 16.8 us
  blocking collectives: 23.1 us -> 28.7 us
  starting transfers between devices: 19.8 us -> 14.4 us
  local copies, waits for them, and re-layouts: 4.24 us -> 1.02 us
  Pallas kernels: 17.4 us -> 15.1 us
    ppermute x8 -> x5, waiting for transfers between devices: 8.62 us -> 16.8 us  [the longest x3 12.6 us: program(): lax.ppermute(own, 'sta', [((j + k) % STA, j) for j in range(STA)])]
    all_to_all x1, blocking collectives: 23.1 us -> 28.7 us  [program(): lax.all_to_all(jnp.broadcast_to(power[None], (DEV, 8, 128)), ('src', 'sta...]
    ppermute x8 -> x5, starting transfers between devices: 8.66 us -> 3.21 us  [the longest x1 1.29 us: program(): halo = lax.ppermute(near, 'src', pairs)]
    unnamed x8 -> x0, local copies, waits for them, and re-layouts: 3.2 us -> none
    pallas_call x4, Pallas kernels: 17.4 us -> 15.1 us  [the longest x1 11.3 us: program(): call(beams, shape((4, 2, 1, 128)), [SMEM] + [VMEM] * 4, [pltpu.VMEM((ROWS...]
  transfers between devices with their start and end apart: 9 -> 6, of which waited for: 4 -> 3; matrix products, arithmetic and copies ran while one was open for 0% -> 0% of each run, Pallas kernels for 1% -> 1%
where the time goes in v3:
time: 77.1 us; the launch traced here: 76.2 us
  blocking collectives  28.7 us (37%)
  waiting for transfers between devices  16.8 us (22%)
  Pallas kernels  15.1 us (20%)
  starting transfers between devices  14.4 us (19%)
  local copies, waits for them, and re-layouts  1.02 us (1%)
    all_to_all x1, blocking collectives, program(): lax.all_to_all(jnp.broadcast_to(power[None], (DEV, 8, 128)), ('src', 'sta...  28.7 us
    ppermute x3, waiting for transfers between devices, program(): lax.ppermute(own, 'sta', [((j + k) % STA, j) for j in range(STA)])  12.6 us
    pallas_call x1, Pallas kernels, program(): call(beams, shape((4, 2, 1, 128)), [SMEM] + [VMEM] * 4, [pltpu.VMEM((ROWS...  11.3 us
    all_to_all x1, starting transfers between devices, program(): received = lax.all_to_all(chunks, ('src', 'sta'), 0, 0, tiled=True)  11.2 us
    ppermute x1, waiting for transfers between devices, program(): halo = lax.ppermute(near, 'src', pairs)  4.19 us
    pallas_call x1, Pallas kernels, program(): call(prologue, [shape((ST, 384)), shape((STA, ROWS, 128), BF16)], [SMEM]...  1.77 us
  transfers between devices with their start and end apart: 6, of which 3 were waited for; matrix products, arithmetic and copies ran while one was open for 0% of the time, Pallas kernels for 1%

profile of v3, /device:TPU:0, one launch (start us, length us, event | category | flops | bytes accessed | tf_op | source)
XLA Modules:
  0.0 76.2 jit_solution(18177690236251978420)
XLA Ops:
  0.0 0.1 pad_add_fusion.where
  0.1 1.8 %shard_map.46 = (f32[64,384]{1,0:T(8,128)S(1)}, bf16[4,24,128]{2,1,0:T(8,128)(2,1)S(1)}) custom-call(s32[2]{0:T(128)S(1)} %pad_add_fusion.where, f32[64,258]{1,0:T(8,128)} %trace.1, f32[64,258]{1,0:T(8,128)} %quad.1, f32[1,64]{1,0:T(1,128)} %bitcast.8, s32[64,128]{1,0:T(8,128)} %bitcast.7), custom_call_target="tpu_custom_call" | custom-call | tf_op jit(solution)/shard_map/pallas_call | solution.py:186
  1.9 1.0 %broadcast_in_dim.17 = bf16[32,4,24,128]{3,2,1,0:T(8,128)(2,1)} broadcast(bf16[4,24,128]{2,1,0:T(8,128)(2,1)S(1)} %get-tuple-element.10), dimensions={1,2,3} | broadcast | bytes 811008 | tf_op jit(solution)/shard_map/broadcast_in_dim | solution.py:201
  2.8 11.2 %all-to-all-start = ((bf16[128,24,128]{2,1,0:T(8,128)(2,1)}), bf16[128,24,128]{2,1,0:T(8,128)(2,1)S(1)}, u32[]{:S(2)}, u32[]{:S(2)}) async-start(bf16[128,24,128]{2,1,0:T(8,128)(2,1)} %bitcast.4), calls=%async_computation | async-start | bytes 1572864 | tf_op jit(solution)/shard_map/all_to_all | solution.py:202
  14.0 0.7 collective-permute-start
  14.8 0.4 collective-permute-start.1
  15.2 0.1 collective-permute-start.2
  15.3 9.5 %collective-permute-done.e1 = f32[64,384]{1,0:T(8,128)S(1)} collective-permute-done((f32[64,384]{1,0:T(8,128)S(1)}, f32[64,384]{1,0:T(8,128)S(1)}, u32[]{:S(2)}, u32[]{:S(2)}) %collective-permute-start) | collective-permute-done | bytes 98336 | tf_op jit(solution)/shard_map/ppermute | solution.py:200
  24.8 3.1 %collective-permute-done.1.e2 = f32[64,384]{1,0:T(8,128)S(1)} collective-permute-done((f32[64,384]{1,0:T(8,128)S(1)}, f32[64,384]{1,0:T(8,128)S(1)}, u32[]{:S(2)}, u32[]{:S(2)}) %collective-permute-start.1) | collective-permute-done | bytes 98336 | tf_op jit(solution)/shard_map/ppermute | solution.py:200
  27.9 0.0 collective-permute-done.2.e3
  27.9 0.8 shard_map.47
  28.7 1.3 %collective-permute-start.3 = (f32[64,256]{1,0:T(8,128)S(1)}, f32[64,256]{1,0:T(8,128)S(1)}, u32[]{:S(2)}, u32[]{:S(2)}) collective-permute-start(f32[64,256]{1,0:T(8,128)S(1)} %get-tuple-element.13), channel_id=1, source_target_pairs={{4,0},{8,4},{12,8},{16,12},{20,16},{24,20},{28,24},{32,28},{36,32}... | collective-permute-start | bytes 196616 | tf_op jit(solution)/shard_map/ppermute | solution.py:211
  30.0 0.7 collective-permute-start.4
  30.7 4.2 %collective-permute-done.3.halo = f32[64,256]{1,0:T(8,128)S(1)} collective-permute-done((f32[64,256]{1,0:T(8,128)S(1)}, f32[64,256]{1,0:T(8,128)S(1)}, u32[]{:S(2)}, u32[]{:S(2)}) %collective-permute-start.3) | collective-permute-done | bytes 65568 | tf_op jit(solution)/shard_map/ppermute | solution.py:211
  34.8 0.0 collective-permute-done.4.far_halo
  34.8 0.0 all-to-all-done.received
  34.8 11.3 %shard_map.48 = f32[4,2,1,128]{3,2,1,0:T(1,128)S(1)} custom-call(s32[2]{0:T(128)S(1)} %pad_add_fusion.where, bf16[128,24,128]{2,1,0:T(8,128)(2,1)S(1)} %all-to-all-done.received, f32[384,256]{1,0:T(8,128)S(1)} %get-tuple-element.12.main, f32[64,256]{1,0:T(8,128)S(1)} %collective-permute-done.3.halo, f32[64,256]{1,0:T(8,128)S(1)} %collective-permute-done.4.far_halo), custom_call_target="tpu_custom_call" | custom-call | tf_op jit(solution)/shard_map/pallas_call | solution.py:213
  46.2 28.7 %all_to_all.10.parts = f32[128,8,128]{2,1,0:T(8,128)S(1)} all-to-all(f32[128,8,128]{2,1,0:T(8,128)S(1)} %broadcast_in_dim.19), channel_id=1, replica_groups=mesh['src'=32,'sta'=4] {'src','sta'}, dimensions={0} | all-to-all | bytes 1048576 | tf_op jit(solution)/shard_map/all_to_all | solution.py:224
  74.9 1.3 %shard_map.49 = f32[2,128]{1,0:T(2,128)} custom-call(s32[2]{0:T(128)S(1)} %pad_add_fusion.where, f32[128,8,128]{2,1,0:T(8,128)S(1)} %all_to_all.10.parts), custom_call_target="tpu_custom_call" | custom-call | tf_op jit(solution)/shard_map/pallas_call | solution.py:225
  (1 shorter events, 0.0 us)
Async XLA Ops:
  2.8 32.0 %all-to-all-start = ((bf16[128,24,128]{2,1,0:T(8,128)(2,1)}), bf16[128,24,128]{2,1,0:T(8,128)(2,1)S(1)}, u32[]{:S(2)}, u32[]{:S(2)}) async-start(bf16[128,24,128]{2,1,0:T(8,128)(2,1)} %bitcast.4), calls=%async_computation | async-start | bytes 1572864 | tf_op jit(solution)/shard_map/all_to_all | solution.py:202
  14.0 10.8 %collective-permute-start = (f32[64,384]{1,0:T(8,128)S(1)}, f32[64,384]{1,0:T(8,128)S(1)}, u32[]{:S(2)}, u32[]{:S(2)}) collective-permute-start(f32[64,384]{1,0:T(8,128)S(1)} %get-tuple-element.11.e0), channel_id=1, source_target_pairs={{1,0},{2,1},{3,2},{0,3},{5,4},{6,5},{7,6},{4,7},{9,8},{10,9},{11,1... | collective-permute-start | bytes 294920 | tf_op jit(solution)/shard_map/ppermute | solution.py:200
  14.8 13.2 %collective-permute-start.1 = (f32[64,384]{1,0:T(8,128)S(1)}, f32[64,384]{1,0:T(8,128)S(1)}, u32[]{:S(2)}, u32[]{:S(2)}) collective-permute-start(f32[64,384]{1,0:T(8,128)S(1)} %get-tuple-element.11.e0), channel_id=1, source_target_pairs={{2,0},{3,1},{0,2},{1,3},{6,4},{7,5},{4,6},{5,7},{10,8},{11,9},{8,1... | collective-permute-start | bytes 294920 | tf_op jit(solution)/shard_map/ppermute | solution.py:200
  15.2 12.8 %collective-permute-start.2 = (f32[64,384]{1,0:T(8,128)S(1)}, f32[64,384]{1,0:T(8,128)S(1)}, u32[]{:S(2)}, u32[]{:S(2)}) collective-permute-start(f32[64,384]{1,0:T(8,128)S(1)} %get-tuple-element.11.e0), channel_id=1, source_target_pairs={{3,0},{0,1},{1,2},{2,3},{7,4},{4,5},{5,6},{6,7},{11,8},{8,9},{9,10... | collective-permute-start | bytes 294920 | tf_op jit(solution)/shard_map/ppermute | solution.py:200
  28.7 6.2 %collective-permute-start.3 = (f32[64,256]{1,0:T(8,128)S(1)}, f32[64,256]{1,0:T(8,128)S(1)}, u32[]{:S(2)}, u32[]{:S(2)}) collective-permute-start(f32[64,256]{1,0:T(8,128)S(1)} %get-tuple-element.13), channel_id=1, source_target_pairs={{4,0},{8,4},{12,8},{16,12},{20,16},{24,20},{28,24},{32,28},{36,32}... | collective-permute-start | bytes 196616 | tf_op jit(solution)/shard_map/ppermute | solution.py:211
  30.0 4.9 %collective-permute-start.4 = (f32[64,256]{1,0:T(8,128)S(1)}, f32[64,256]{1,0:T(8,128)S(1)}, u32[]{:S(2)}, u32[]{:S(2)}) collective-permute-start(f32[64,256]{1,0:T(8,128)S(1)} %get-tuple-element.14), channel_id=1, source_target_pairs={{64,60},{60,64},{65,61},{61,65},{66,62},{62,66},{67,63},{63,67}} | collective-permute-start | bytes 196616 | tf_op jit(solution)/shard_map/ppermute | solution.py:212

commit v4 on v3

--- a/solution.py
+++ b/solution.py
@@ -12,7 +12,6 @@
 F32 = jnp.float32
 BF16 = jnp.bfloat16
 VMEM = pl.BlockSpec(memory_space=pltpu.VMEM)
-SMEM = pl.BlockSpec(memory_space=pltpu.SMEM)
 
 SRC = 32
 STA = 4
@@ -30,7 +29,7 @@
 HALF = SRC // STEPS * STA
 
 
-def prologue(where, trace, quad, gains, lags, own, chunk, tr_in, qd_in, ga_in, lg_in, sem):
+def prologue(trace, quad, gains, lags, own, chunk, tr_in, qd_in, ga_in, lg_in, sem):
     copies = [
         pltpu.make_async_copy(a, b, sem.at[k])
         for k, (a, b) in enumerate(((trace, tr_in), (quad, qd_in), (gains, ga_in), (lags, lg_in)))
@@ -54,7 +53,7 @@
     row = lax.broadcasted_iota(jnp.int32, (8, 128), 0)
     lane = lax.broadcasted_iota(jnp.int32, (8, 128), 1)
     sums = jnp.where(row == 0, hi, jnp.where(row == 1, mid, jnp.where(row == 2, low, 0.0)))
-    sums = jnp.where(lane // ST == where[1] % 2, sums, 0.0)
+    sums = jnp.where(lane // ST == lax.axis_index("sta") % 2, sums, 0.0)
     lag = lg_in[...].astype(F32)
     lag = jnp.concatenate([lag, lag], axis=0).T
     for j in range(STA):
@@ -62,18 +61,18 @@
         chunk[j] = jnp.concatenate([body, sums], axis=0).astype(BF16)
 
 
-def turn(where, e0, e1, e2, e3, main, near, far, tall):
+def turn(e0, e1, e2, e3, main, near, far, tall):
     for k, e in enumerate((e0, e1, e2, e3)):
-        at = pl.multiple_of((where[1] + k) % STA * ST, ST)
+        at = pl.multiple_of((lax.axis_index("sta") + k) % STA * ST, ST)
         tall[pl.ds(at, ST), :] = e[...]
     main[...] = tall[...].T
     first, last = main[0:64, :], main[BLK - 64 : BLK, :]
-    low_half = where[0] < SRC // STEPS
+    low_half = lax.axis_index("src") < SRC // STEPS
     near[...] = jnp.where(low_half, first, last)
     far[...] = jnp.where(low_half, last, first)
 
 
-def beams(where, received, main, halo, far_halo, power, line, weighted, lagged):
+def beams(received, main, halo, far_halo, power, line, weighted, lagged):
     halves = []
     for half in range(2):
         acc = jnp.zeros((8, 128), F32)
@@ -87,7 +86,7 @@
     def weigh(energy):
         return (gain * (energy - baseline)).astype(BF16).astype(F32)
 
-    src = where[0]
+    src = lax.axis_index("src")
     middle = SRC // STEPS
     edge = weigh(halo[...] + far_halo[...])
 
@@ -142,8 +141,8 @@
     lax.fori_loop(0, 4, one, 0)
 
 
-def finish(where, parts, out, sums):
-    src = where[0]
+def finish(parts, out, sums):
+    src = lax.axis_index("src")
     lane = lax.broadcasted_iota(jnp.int32, (1, 128), 1)
     for k in range(STEPS):
         peak = None
@@ -181,12 +180,11 @@
 
 
 def program(trace, quadrature, gains, lags):
-    where = jnp.stack([lax.axis_index("src"), lax.axis_index("sta")]).astype(jnp.int32)
     inputs = [pltpu.with_memory_space_constraint(x, pltpu.HBM) for x in (trace, quadrature, gains[None], lags.T)]
     own, chunk = call(
         prologue,
         [shape((ST, 384)), shape((STA, ROWS, 128), BF16)],
-        [SMEM] + [pl.BlockSpec(memory_space=pltpu.HBM)] * 4,
+        [pl.BlockSpec(memory_space=pltpu.HBM)] * 4,
         [
             pltpu.VMEM((ST, BLK), F32),
             pltpu.VMEM((ST, BLK), F32),
@@ -194,7 +192,7 @@
             pltpu.VMEM((ST, CPD), jnp.int32),
             pltpu.SemaphoreType.DMA((4,)),
         ],
-    )(where, *inputs)
+    )(*inputs)
     blocks = [own]
     for k in range(1, STA):
         blocks.append(lax.ppermute(own, "sta", [((j + k) % STA, j) for j in range(STA)]))
@@ -203,9 +201,9 @@
     main, near, far = call(
         turn,
         [shape((384, STATIONS)), shape((64, STATIONS)), shape((64, STATIONS))],
-        [SMEM] + [VMEM] * 4,
+        [VMEM] * 4,
         [pltpu.VMEM((STATIONS, 384), F32)],
-    )(where, *blocks)
+    )(*blocks)
     middle = SRC // STEPS
     pairs = [(i + 1, i) for i in range(middle - 1)] + [(i - 1, i) for i in range(middle + 1, SRC)]
     halo = lax.ppermute(near, "src", pairs)
@@ -213,16 +211,16 @@
     power = call(
         beams,
         shape((4, 2, 1, 128)),
-        [SMEM] + [VMEM] * 4,
+        [VMEM] * 4,
         [
             pltpu.VMEM((ROWS_IN, STATIONS), F32),
             pltpu.VMEM((16, ROWS_OUT + 48, STATIONS), BF16),
             pltpu.VMEM((4, STATIONS, 256), BF16),
         ],
-    )(where, received, main, halo, far_halo)
+    )(received, main, halo, far_halo)
     power = power.reshape(8, 128)
     parts = lax.all_to_all(jnp.broadcast_to(power[None], (DEV, 8, 128)), ("src", "sta"), 0, 0, tiled=True)
-    return call(finish, shape((STEPS, CPD)), [SMEM, VMEM], [pltpu.VMEM((32, 128), F32)])(where, parts)
+    return call(finish, shape((STEPS, CPD)), [VMEM], [pltpu.VMEM((32, 128), F32)])(parts)
 
 
 def solution(mesh):

time: 77.1 us -> 74.9 us (0.971)
  Pallas kernels: 15.1 us -> 12.9 us
    pallas_call x3, Pallas kernels: 14.3 us -> 12.7 us  [the longest x1 10.7 us: program(): call(beams, shape((4, 2, 1, 128)), [VMEM] * 4, [pltpu.VMEM((ROWS_IN, STAT...]
  transfers between devices with their start and end apart: 6 -> 6, of which waited for: 3 -> 3; matrix products, arithmetic and copies ran while one was open for 0% -> 0% of each run, Pallas kernels for 1% -> 0%
where the time goes in v4:
time: 74.9 us; the launch traced here: 73.9 us
  blocking collectives  28.7 us (38%)
  waiting for transfers between devices  16.8 us (22%)
  starting transfers between devices  14.4 us (19%)
  Pallas kernels  12.9 us (17%)
  local copies, waits for them, and re-layouts  1.02 us (1%)
    all_to_all x1, blocking collectives, program(): lax.all_to_all(jnp.broadcast_to(power[None], (DEV, 8, 128)), ('src', 'sta...  28.7 us
    ppermute x3, waiting for transfers between devices, program(): lax.ppermute(own, 'sta', [((j + k) % STA, j) for j in range(STA)])  12.6 us
    all_to_all x1, starting transfers between devices, program(): received = lax.all_to_all(chunks, ('src', 'sta'), 0, 0, tiled=True)  11.2 us
    pallas_call x1, Pallas kernels, program(): call(beams, shape((4, 2, 1, 128)), [VMEM] * 4, [pltpu.VMEM((ROWS_IN, STAT...  10.7 us
    ppermute x1, waiting for transfers between devices, program(): halo = lax.ppermute(near, 'src', pairs)  4.19 us
  transfers between devices with their start and end apart: 6, of which 3 were waited for; matrix products, arithmetic and copies ran while one was open for 0% of the time, Pallas kernels for 0%

profile of v4, /device:TPU:0, one launch (start us, length us, event | category | flops | bytes accessed | tf_op | source)
XLA Modules:
  0.0 73.9 jit_solution(7899788468426715701)
XLA Ops:
  0.0 1.2 %shard_map.46 = (f32[64,384]{1,0:T(8,128)S(1)}, bf16[4,24,128]{2,1,0:T(8,128)(2,1)S(1)}) custom-call(f32[64,258]{1,0:T(8,128)} %trace.1, f32[64,258]{1,0:T(8,128)} %quad.1, f32[1,64]{1,0:T(1,128)} %bitcast.6, s32[64,128]{1,0:T(8,128)} %bitcast.5), custom_call_target="tpu_custom_call" | custom-call | tf_op jit(solution)/shard_map/pallas_call | solution.py:184
  1.2 1.0 %broadcast_in_dim.17 = bf16[32,4,24,128]{3,2,1,0:T(8,128)(2,1)} broadcast(bf16[4,24,128]{2,1,0:T(8,128)(2,1)S(1)} %get-tuple-element.10), dimensions={1,2,3} | broadcast | bytes 811008 | tf_op jit(solution)/shard_map/broadcast_in_dim | solution.py:199
  2.2 11.2 %all-to-all-start = ((bf16[128,24,128]{2,1,0:T(8,128)(2,1)}), bf16[128,24,128]{2,1,0:T(8,128)(2,1)S(1)}, u32[]{:S(2)}, u32[]{:S(2)}) async-start(bf16[128,24,128]{2,1,0:T(8,128)(2,1)} %bitcast.2), calls=%async_computation | async-start | bytes 1572864 | tf_op jit(solution)/shard_map/all_to_all | solution.py:200
  13.4 0.7 %collective-permute-start = (f32[64,384]{1,0:T(8,128)S(1)}, f32[64,384]{1,0:T(8,128)S(1)}, u32[]{:S(2)}, u32[]{:S(2)}) collective-permute-start(f32[64,384]{1,0:T(8,128)S(1)} %get-tuple-element.11.e0), channel_id=1, source_target_pairs={{1,0},{2,1},{3,2},{0,3},{5,4},{6,5},{7,6},{4,7},{9,8},{10,9},{11,1... | collective-permute-start | bytes 294920 | tf_op jit(solution)/shard_map/ppermute | solution.py:198
  14.2 0.4 collective-permute-start.1
  14.5 0.1 collective-permute-start.2
  14.7 9.5 %collective-permute-done.e1 = f32[64,384]{1,0:T(8,128)S(1)} collective-permute-done((f32[64,384]{1,0:T(8,128)S(1)}, f32[64,384]{1,0:T(8,128)S(1)}, u32[]{:S(2)}, u32[]{:S(2)}) %collective-permute-start) | collective-permute-done | bytes 98336 | tf_op jit(solution)/shard_map/ppermute | solution.py:198
  24.2 3.1 %collective-permute-done.1.e2 = f32[64,384]{1,0:T(8,128)S(1)} collective-permute-done((f32[64,384]{1,0:T(8,128)S(1)}, f32[64,384]{1,0:T(8,128)S(1)}, u32[]{:S(2)}, u32[]{:S(2)}) %collective-permute-start.1) | collective-permute-done | bytes 98336 | tf_op jit(solution)/shard_map/ppermute | solution.py:198
  27.3 0.0 collective-permute-done.2.e3
  27.3 0.2 shard_map.47
  27.5 1.3 %collective-permute-start.3 = (f32[64,256]{1,0:T(8,128)S(1)}, f32[64,256]{1,0:T(8,128)S(1)}, u32[]{:S(2)}, u32[]{:S(2)}) collective-permute-start(f32[64,256]{1,0:T(8,128)S(1)} %get-tuple-element.13), channel_id=1, source_target_pairs={{4,0},{8,4},{12,8},{16,12},{20,16},{24,20},{28,24},{32,28},{36,32}... | collective-permute-start | bytes 196616 | tf_op jit(solution)/shard_map/ppermute | solution.py:209
  28.8 0.7 collective-permute-start.4
  29.5 4.2 %collective-permute-done.3.halo = f32[64,256]{1,0:T(8,128)S(1)} collective-permute-done((f32[64,256]{1,0:T(8,128)S(1)}, f32[64,256]{1,0:T(8,128)S(1)}, u32[]{:S(2)}, u32[]{:S(2)}) %collective-permute-start.3) | collective-permute-done | bytes 65568 | tf_op jit(solution)/shard_map/ppermute | solution.py:209
  33.7 0.0 collective-permute-done.4.far_halo
  33.7 0.0 all-to-all-done.received
  33.7 10.7 %shard_map.48 = f32[4,2,1,128]{3,2,1,0:T(1,128)S(1)} custom-call(bf16[128,24,128]{2,1,0:T(8,128)(2,1)S(1)} %all-to-all-done.received, f32[384,256]{1,0:T(8,128)S(1)} %get-tuple-element.12.main, f32[64,256]{1,0:T(8,128)S(1)} %collective-permute-done.3.halo, f32[64,256]{1,0:T(8,128)S(1)} %collective-permute-done.4.far_halo), custom_call_target="tpu_custom_call" | custom-call | tf_op jit(solution)/shard_map/pallas_call | solution.py:211
  44.5 28.7 %all_to_all.10.parts = f32[128,8,128]{2,1,0:T(8,128)S(1)} all-to-all(f32[128,8,128]{2,1,0:T(8,128)S(1)} %broadcast_in_dim.19), channel_id=1, replica_groups=mesh['src'=32,'sta'=4] {'src','sta'}, dimensions={0} | all-to-all | bytes 1048576 | tf_op jit(solution)/shard_map/all_to_all | solution.py:222
  73.2 0.7 shard_map.49
  (1 shorter events, 0.0 us)
Async XLA Ops:
  2.2 31.5 %all-to-all-start = ((bf16[128,24,128]{2,1,0:T(8,128)(2,1)}), bf16[128,24,128]{2,1,0:T(8,128)(2,1)S(1)}, u32[]{:S(2)}, u32[]{:S(2)}) async-start(bf16[128,24,128]{2,1,0:T(8,128)(2,1)} %bitcast.2), calls=%async_computation | async-start | bytes 1572864 | tf_op jit(solution)/shard_map/all_to_all | solution.py:200
  13.4 10.8 %collective-permute-start = (f32[64,384]{1,0:T(8,128)S(1)}, f32[64,384]{1,0:T(8,128)S(1)}, u32[]{:S(2)}, u32[]{:S(2)}) collective-permute-start(f32[64,384]{1,0:T(8,128)S(1)} %get-tuple-element.11.e0), channel_id=1, source_target_pairs={{1,0},{2,1},{3,2},{0,3},{5,4},{6,5},{7,6},{4,7},{9,8},{10,9},{11,1... | collective-permute-start | bytes 294920 | tf_op jit(solution)/shard_map/ppermute | solution.py:198
  14.2 13.2 %collective-permute-start.1 = (f32[64,384]{1,0:T(8,128)S(1)}, f32[64,384]{1,0:T(8,128)S(1)}, u32[]{:S(2)}, u32[]{:S(2)}) collective-permute-start(f32[64,384]{1,0:T(8,128)S(1)} %get-tuple-element.11.e0), channel_id=1, source_target_pairs={{2,0},{3,1},{0,2},{1,3},{6,4},{7,5},{4,6},{5,7},{10,8},{11,9},{8,1... | collective-permute-start | bytes 294920 | tf_op jit(solution)/shard_map/ppermute | solution.py:198
  14.5 12.8 %collective-permute-start.2 = (f32[64,384]{1,0:T(8,128)S(1)}, f32[64,384]{1,0:T(8,128)S(1)}, u32[]{:S(2)}, u32[]{:S(2)}) collective-permute-start(f32[64,384]{1,0:T(8,128)S(1)} %get-tuple-element.11.e0), channel_id=1, source_target_pairs={{3,0},{0,1},{1,2},{2,3},{7,4},{4,5},{5,6},{6,7},{11,8},{8,9},{9,10... | collective-permute-start | bytes 294920 | tf_op jit(solution)/shard_map/ppermute | solution.py:198
  27.5 6.2 %collective-permute-start.3 = (f32[64,256]{1,0:T(8,128)S(1)}, f32[64,256]{1,0:T(8,128)S(1)}, u32[]{:S(2)}, u32[]{:S(2)}) collective-permute-start(f32[64,256]{1,0:T(8,128)S(1)} %get-tuple-element.13), channel_id=1, source_target_pairs={{4,0},{8,4},{12,8},{16,12},{20,16},{24,20},{28,24},{32,28},{36,32}... | collective-permute-start | bytes 196616 | tf_op jit(solution)/shard_map/ppermute | solution.py:209
  28.8 4.9 %collective-permute-start.4 = (f32[64,256]{1,0:T(8,128)S(1)}, f32[64,256]{1,0:T(8,128)S(1)}, u32[]{:S(2)}, u32[]{:S(2)}) collective-permute-start(f32[64,256]{1,0:T(8,128)S(1)} %get-tuple-element.14), channel_id=1, source_target_pairs={{64,60},{60,64},{65,61},{61,65},{66,62},{62,66},{67,63},{63,67}} | collective-permute-start | bytes 196616 | tf_op jit(solution)/shard_map/ppermute | solution.py:210

commit v5 on v4

--- a/solution.py
+++ b/solution.py
@@ -24,7 +24,7 @@
 ROWS_OUT = 264
 ROWS_IN = ROWS_OUT + LAGS
 CPD = 128
-ROWS = 24
+WIDE = 9 * 128
 SAMPLES = BLK * SRC
 HALF = SRC // STEPS * STA
 
@@ -46,19 +46,19 @@
     own[:, BLK:] = gain[:, : 384 - BLK]
     total = jnp.sum(energy, axis=1, keepdims=True)
     total = jnp.broadcast_to(total, (ST, 128))
-    total = jnp.concatenate([total, total], axis=0).T[:8]
+    total = jnp.concatenate([total, total], axis=0).T[:2]
     hi = total.astype(BF16).astype(F32)
     mid = (total - hi).astype(BF16).astype(F32)
     low = total - hi - mid
-    row = lax.broadcasted_iota(jnp.int32, (8, 128), 0)
-    lane = lax.broadcasted_iota(jnp.int32, (8, 128), 1)
-    sums = jnp.where(row == 0, hi, jnp.where(row == 1, mid, jnp.where(row == 2, low, 0.0)))
-    sums = jnp.where(lane // ST == lax.axis_index("sta") % 2, sums, 0.0)
+    row = lax.broadcasted_iota(jnp.int32, (2, 128), 0)
+    lane = lax.broadcasted_iota(jnp.int32, (2, 128), 1)
+    sums = jnp.where(row == 0, jnp.where(lane < ST, hi, mid), jnp.where(lane < ST, low, 0.0))
     lag = lg_in[...].astype(F32)
     lag = jnp.concatenate([lag, lag], axis=0).T
     for j in range(STA):
         body = jnp.where(lane[:1] < ST, lag[32 * j : 32 * j + 16], lag[32 * j + 16 : 32 * j + 32])
-        chunk[j] = jnp.concatenate([body, sums], axis=0).astype(BF16)
+        pieces = [body[2 * k : 2 * k + 2] for k in range(8)] + [sums]
+        chunk[j] = jnp.concatenate(pieces, axis=1).astype(BF16)
 
 
 def turn(e0, e1, e2, e3, main, near, far, tall):
@@ -72,14 +72,16 @@
     far[...] = jnp.where(low_half, last, first)
 
 
-def beams(received, main, halo, far_halo, power, line, weighted, lagged):
-    halves = []
-    for half in range(2):
-        acc = jnp.zeros((8, 128), F32)
+def beams(received, main, halo, far_halo, power, line, weighted, lagged, opened):
+    lane = lax.broadcasted_iota(jnp.int32, (1, 128), 1)
+    totals = []
+    for j in range(STA):
+        acc = jnp.zeros((2, 128), F32)
         for i in range(SRC):
-            for j in (2 * half, 2 * half + 1):
-                acc = acc + received[STA * i + j, 16:24, :].astype(F32)
-        halves.append(jnp.sum(acc, axis=0, keepdims=True))
+            acc = acc + received[STA * i + j, :, 1024:].astype(F32)
+        acc = acc[0:1] + acc[1:2]
+        totals.append(acc + pltpu.roll(acc, ST, 1))
+    halves = [jnp.where(lane < ST, totals[0], totals[1]), jnp.where(lane < ST, totals[2], totals[3])]
     baseline = jnp.concatenate(halves, axis=1) / SAMPLES
     gain = main[BLK : BLK + 1, :]
 
@@ -107,8 +109,12 @@
     row = lax.broadcasted_iota(jnp.int32, (ROWS_OUT, 256), 0)
     inside = jnp.logical_and(row >= start, row < stop)
     for j in range(STA):
-        part = jnp.concatenate([received[STA * i + j, 0:16, :] for i in range(SRC)], axis=0)
-        part = part.astype(F32).T.astype(BF16)
+        for i in range(SRC):
+            for k in range(8):
+                opened[16 * i + 2 * k : 16 * i + 2 * k + 2, :] = received[
+                    STA * i + j, :, 128 * k : 128 * k + 128
+                ].astype(F32)
+        part = opened[...].T.astype(BF16)
         for group in range(4):
             lagged[group, ST * j : ST * j + ST, :] = part[
                 ST * (group // 2) : ST * (group // 2) + ST, 256 * (group % 2) : 256 * (group % 2) + 256
@@ -183,7 +189,7 @@
     inputs = [pltpu.with_memory_space_constraint(x, pltpu.HBM) for x in (trace, quadrature, gains[None], lags.T)]
     own, chunk = call(
         prologue,
-        [shape((ST, 384)), shape((STA, ROWS, 128), BF16)],
+        [shape((ST, 384)), shape((STA, 2, WIDE), BF16)],
         [pl.BlockSpec(memory_space=pltpu.HBM)] * 4,
         [
             pltpu.VMEM((ST, BLK), F32),
@@ -196,7 +202,7 @@
     blocks = [own]
     for k in range(1, STA):
         blocks.append(lax.ppermute(own, "sta", [((j + k) % STA, j) for j in range(STA)]))
-    chunks = jnp.broadcast_to(chunk[None], (SRC, STA, ROWS, 128)).reshape(DEV, ROWS, 128)
+    chunks = jnp.broadcast_to(chunk[None], (SRC, STA, 2, WIDE)).reshape(DEV, 2, WIDE)
     received = lax.all_to_all(chunks, ("src", "sta"), 0, 0, tiled=True)
     main, near, far = call(
         turn,
@@ -216,6 +222,7 @@
             pltpu.VMEM((ROWS_IN, STATIONS), F32),
             pltpu.VMEM((16, ROWS_OUT + 48, STATIONS), BF16),
             pltpu.VMEM((4, STATIONS, 256), BF16),
+            pltpu.VMEM((512, 128), F32),
         ],
     )(received, main, halo, far_halo)
     power = power.reshape(8, 128)

time: 74.9 us -> 73.3 us (0.979)
  waiting for transfers between devices: 16.8 us -> 14.7 us
    ppermute x3, waiting for transfers between devices: 12.6 us -> 10.5 us  [program(): lax.ppermute(own, 'sta', [((j + k) % STA, j) for j in range(STA)])]
where the time goes in v5:
time: 73.3 us; the launch traced here: 72.3 us
  blocking collectives  28.7 us (39%)
  waiting for transfers between devices  14.7 us (20%)
  starting transfers between devices  14.4 us (20%)
  Pallas kernels  13.2 us (18%)
  local copies, waits for them, and re-layouts  1.16 us (2%)
    all_to_all x1, blocking collectives, program(): lax.all_to_all(jnp.broadcast_to(power[None], (DEV, 8, 128)), ('src', 'sta...  28.7 us
    all_to_all x1, starting transfers between devices, program(): received = lax.all_to_all(chunks, ('src', 'sta'), 0, 0, tiled=True)  11.2 us
    pallas_call x1, Pallas kernels, program(): call(beams, shape((4, 2, 1, 128)), [VMEM] * 4, [pltpu.VMEM((ROWS_IN, STAT...  11.1 us
    ppermute x3, waiting for transfers between devices, program(): lax.ppermute(own, 'sta', [((j + k) % STA, j) for j in range(STA)])  10.5 us
    ppermute x1, waiting for transfers between devices, program(): halo = lax.ppermute(near, 'src', pairs)  4.19 us
  transfers between devices with their start and end apart: 6, of which 3 were waited for; matrix products, arithmetic and copies ran while one was open for 0% of the time, Pallas kernels for 0%

profile of v5, /device:TPU:0, one launch (start us, length us, event | category | flops | bytes accessed | tf_op | source)
XLA Modules:
  0.0 72.3 jit_solution(4501817692229444196)
XLA Ops:
  0.0 1.2 %shard_map.46 = (f32[64,384]{1,0:T(8,128)S(1)}, bf16[4,2,1152]{2,1,0:T(2,128)(2,1)S(1)}) custom-call(f32[64,258]{1,0:T(8,128)} %trace.1, f32[64,258]{1,0:T(8,128)} %quad.1, f32[1,64]{1,0:T(1,128)} %bitcast.6, s32[64,128]{1,0:T(8,128)} %bitcast.5), custom_call_target="tpu_custom_call" | custom-call | tf_op jit(solution)/shard_map/pallas_call | solution.py:190
  1.2 1.1 %broadcast_in_dim.17 = bf16[32,4,2,1152]{3,2,1,0:T(2,128)(2,1)} broadcast(bf16[4,2,1152]{2,1,0:T(2,128)(2,1)S(1)} %get-tuple-element.10), dimensions={1,2,3} | broadcast | bytes 608256 | tf_op jit(solution)/shard_map/broadcast_in_dim | solution.py:205
  2.4 11.2 %all-to-all-start = ((bf16[128,2,1152]{2,1,0:T(2,128)(2,1)}), bf16[128,2,1152]{2,1,0:T(2,128)(2,1)S(1)}, u32[]{:S(2)}, u32[]{:S(2)}) async-start(bf16[128,2,1152]{2,1,0:T(2,128)(2,1)} %bitcast.2), calls=%async_computation | async-start | bytes 1179648 | tf_op jit(solution)/shard_map/all_to_all | solution.py:206
  13.5 0.7 %collective-permute-start = (f32[64,384]{1,0:T(8,128)S(1)}, f32[64,384]{1,0:T(8,128)S(1)}, u32[]{:S(2)}, u32[]{:S(2)}) collective-permute-start(f32[64,384]{1,0:T(8,128)S(1)} %get-tuple-element.11.e0), channel_id=1, source_target_pairs={{1,0},{2,1},{3,2},{0,3},{5,4},{6,5},{7,6},{4,7},{9,8},{10,9},{11,1... | collective-permute-start | bytes 294920 | tf_op jit(solution)/shard_map/ppermute | solution.py:204
  14.3 0.4 collective-permute-start.1
  14.7 0.1 collective-permute-start.2
  14.8 7.4 %collective-permute-done.e1 = f32[64,384]{1,0:T(8,128)S(1)} collective-permute-done((f32[64,384]{1,0:T(8,128)S(1)}, f32[64,384]{1,0:T(8,128)S(1)}, u32[]{:S(2)}, u32[]{:S(2)}) %collective-permute-start) | collective-permute-done | bytes 98336 | tf_op jit(solution)/shard_map/ppermute | solution.py:204
  22.2 3.1 %collective-permute-done.1.e2 = f32[64,384]{1,0:T(8,128)S(1)} collective-permute-done((f32[64,384]{1,0:T(8,128)S(1)}, f32[64,384]{1,0:T(8,128)S(1)}, u32[]{:S(2)}, u32[]{:S(2)}) %collective-permute-start.1) | collective-permute-done | bytes 98336 | tf_op jit(solution)/shard_map/ppermute | solution.py:204
  25.3 0.0 collective-permute-done.2.e3
  25.3 0.2 shard_map.47
  25.6 1.3 %collective-permute-start.3 = (f32[64,256]{1,0:T(8,128)S(1)}, f32[64,256]{1,0:T(8,128)S(1)}, u32[]{:S(2)}, u32[]{:S(2)}) collective-permute-start(f32[64,256]{1,0:T(8,128)S(1)} %get-tuple-element.13), channel_id=1, source_target_pairs={{4,0},{8,4},{12,8},{16,12},{20,16},{24,20},{28,24},{32,28},{36,32}... | collective-permute-start | bytes 196616 | tf_op jit(solution)/shard_map/ppermute | solution.py:215
  26.9 0.7 collective-permute-start.4
  27.5 4.2 %collective-permute-done.3.halo = f32[64,256]{1,0:T(8,128)S(1)} collective-permute-done((f32[64,256]{1,0:T(8,128)S(1)}, f32[64,256]{1,0:T(8,128)S(1)}, u32[]{:S(2)}, u32[]{:S(2)}) %collective-permute-start.3) | collective-permute-done | bytes 65568 | tf_op jit(solution)/shard_map/ppermute | solution.py:215
  31.7 0.0 collective-permute-done.4.far_halo
  31.7 0.0 all-to-all-done.received
  31.7 11.1 %shard_map.48 = f32[4,2,1,128]{3,2,1,0:T(1,128)S(1)} custom-call(bf16[128,2,1152]{2,1,0:T(2,128)(2,1)S(1)} %all-to-all-done.received, f32[384,256]{1,0:T(8,128)S(1)} %get-tuple-element.12.main, f32[64,256]{1,0:T(8,128)S(1)} %collective-permute-done.3.halo, f32[64,256]{1,0:T(8,128)S(1)} %collective-permute-done.4.far_halo), custom_call_target="tpu_custom_call" | custom-call | tf_op jit(solution)/shard_map/pallas_call | solution.py:217
  42.9 28.7 %all_to_all.10.parts = f32[128,8,128]{2,1,0:T(8,128)S(1)} all-to-all(f32[128,8,128]{2,1,0:T(8,128)S(1)} %broadcast_in_dim.19), channel_id=1, replica_groups=mesh['src'=32,'sta'=4] {'src','sta'}, dimensions={0} | all-to-all | bytes 1048576 | tf_op jit(solution)/shard_map/all_to_all | solution.py:229
  71.6 0.7 shard_map.49
  (1 shorter events, 0.0 us)
Async XLA Ops:
  2.4 29.4 %all-to-all-start = ((bf16[128,2,1152]{2,1,0:T(2,128)(2,1)}), bf16[128,2,1152]{2,1,0:T(2,128)(2,1)S(1)}, u32[]{:S(2)}, u32[]{:S(2)}) async-start(bf16[128,2,1152]{2,1,0:T(2,128)(2,1)} %bitcast.2), calls=%async_computation | async-start | bytes 1179648 | tf_op jit(solution)/shard_map/all_to_all | solution.py:206
  13.5 8.7 %collective-permute-start = (f32[64,384]{1,0:T(8,128)S(1)}, f32[64,384]{1,0:T(8,128)S(1)}, u32[]{:S(2)}, u32[]{:S(2)}) collective-permute-start(f32[64,384]{1,0:T(8,128)S(1)} %get-tuple-element.11.e0), channel_id=1, source_target_pairs={{1,0},{2,1},{3,2},{0,3},{5,4},{6,5},{7,6},{4,7},{9,8},{10,9},{11,1... | collective-permute-start | bytes 294920 | tf_op jit(solution)/shard_map/ppermute | solution.py:204
  14.3 11.0 %collective-permute-start.1 = (f32[64,384]{1,0:T(8,128)S(1)}, f32[64,384]{1,0:T(8,128)S(1)}, u32[]{:S(2)}, u32[]{:S(2)}) collective-permute-start(f32[64,384]{1,0:T(8,128)S(1)} %get-tuple-element.11.e0), channel_id=1, source_target_pairs={{2,0},{3,1},{0,2},{1,3},{6,4},{7,5},{4,6},{5,7},{10,8},{11,9},{8,1... | collective-permute-start | bytes 294920 | tf_op jit(solution)/shard_map/ppermute | solution.py:204
  14.7 10.7 %collective-permute-start.2 = (f32[64,384]{1,0:T(8,128)S(1)}, f32[64,384]{1,0:T(8,128)S(1)}, u32[]{:S(2)}, u32[]{:S(2)}) collective-permute-start(f32[64,384]{1,0:T(8,128)S(1)} %get-tuple-element.11.e0), channel_id=1, source_target_pairs={{3,0},{0,1},{1,2},{2,3},{7,4},{4,5},{5,6},{6,7},{11,8},{8,9},{9,10... | collective-permute-start | bytes 294920 | tf_op jit(solution)/shard_map/ppermute | solution.py:204
  25.6 6.2 %collective-permute-start.3 = (f32[64,256]{1,0:T(8,128)S(1)}, f32[64,256]{1,0:T(8,128)S(1)}, u32[]{:S(2)}, u32[]{:S(2)}) collective-permute-start(f32[64,256]{1,0:T(8,128)S(1)} %get-tuple-element.13), channel_id=1, source_target_pairs={{4,0},{8,4},{12,8},{16,12},{20,16},{24,20},{28,24},{32,28},{36,32}... | collective-permute-start | bytes 196616 | tf_op jit(solution)/shard_map/ppermute | solution.py:215
  26.9 4.9 %collective-permute-start.4 = (f32[64,256]{1,0:T(8,128)S(1)}, f32[64,256]{1,0:T(8,128)S(1)}, u32[]{:S(2)}, u32[]{:S(2)}) collective-permute-start(f32[64,256]{1,0:T(8,128)S(1)} %get-tuple-element.14), channel_id=1, source_target_pairs={{64,60},{60,64},{65,61},{61,65},{66,62},{62,66},{67,63},{63,67}} | collective-permute-start | bytes 196616 | tf_op jit(solution)/shard_map/ppermute | solution.py:216

commit v6 on v5

--- a/solution.py
+++ b/solution.py
@@ -20,9 +20,7 @@
 ST = 64
 STATIONS = ST * STA
 HALO = LAGS - 1
-CHAIN = 64
-ROWS_OUT = 264
-ROWS_IN = ROWS_OUT + LAGS
+COPIES = 16
 CPD = 128
 WIDE = 9 * 128
 SAMPLES = BLK * SRC
@@ -72,8 +70,11 @@
     far[...] = jnp.where(low_half, last, first)
 
 
-def beams(received, main, halo, far_halo, power, line, weighted, lagged, opened):
+def beams(received, main, halo, far_halo, power, line, weighted, table, lagged, opened):
+    src = lax.axis_index("src")
+    middle = SRC // STEPS
     lane = lax.broadcasted_iota(jnp.int32, (1, 128), 1)
+    left = lane < ST
     totals = []
     for j in range(STA):
         acc = jnp.zeros((2, 128), F32)
@@ -81,15 +82,13 @@
             acc = acc + received[STA * i + j, :, 1024:].astype(F32)
         acc = acc[0:1] + acc[1:2]
         totals.append(acc + pltpu.roll(acc, ST, 1))
-    halves = [jnp.where(lane < ST, totals[0], totals[1]), jnp.where(lane < ST, totals[2], totals[3])]
+    halves = [jnp.where(left, totals[0], totals[1]), jnp.where(left, totals[2], totals[3])]
     baseline = jnp.concatenate(halves, axis=1) / SAMPLES
     gain = main[BLK : BLK + 1, :]
 
     def weigh(energy):
         return (gain * (energy - baseline)).astype(BF16).astype(F32)
 
-    src = lax.axis_index("src")
-    middle = SRC // STEPS
     edge = weigh(halo[...] + far_halo[...])
 
     @pl.when(src < middle)
@@ -102,49 +101,54 @@
         line[0:HALO, :] = edge[1:64]
         line[HALO : HALO + 264, :] = weigh(main[0:264, :])
 
-    for b in range(16):
-        weighted[b] = line[b : b + ROWS_OUT + 48, :].astype(BF16)
-    start = jnp.where(src == middle, W - (BLK * middle - HALO), 0)
-    stop = jnp.where(src == middle - 1, W - BLK * (middle - 1), jnp.where(src == SRC - 1, BLK - 1, BLK))
-    row = lax.broadcasted_iota(jnp.int32, (ROWS_OUT, 256), 0)
-    inside = jnp.logical_and(row >= start, row < stop)
+    for b in range(COPIES):
+        weighted[b] = line[b : b + 256 + LAGS - COPIES, :].astype(BF16)
+    table[...] = line[256:384, :].T
+    extra = [[jnp.zeros((8, 512), F32) for _ in range(2)] for _ in range(2)]
     for j in range(STA):
         for i in range(SRC):
             for k in range(8):
-                opened[16 * i + 2 * k : 16 * i + 2 * k + 2, :] = received[
+                opened[j, 16 * i + 2 * k : 16 * i + 2 * k + 2, :] = received[
                     STA * i + j, :, 128 * k : 128 * k + 128
                 ].astype(F32)
-        part = opened[...].T.astype(BF16)
-        for group in range(4):
-            lagged[group, ST * j : ST * j + ST, :] = part[
-                ST * (group // 2) : ST * (group // 2) + ST, 256 * (group % 2) : 256 * (group % 2) + 256
-            ]
-
-    def one(group, carry):
-        lag = lagged[group]
-
-        def add(step, total):
-            base = pl.multiple_of(step * CHAIN, 16)
-            picks, shifted = [], []
-            for b in range(CHAIN):
-                value = (base + b).astype(F32).astype(BF16) if CHAIN < LAGS else BF16(b)
-                picks.append(jnp.where(lag == value, BF16(1), BF16(0)))
-                shifted.append(weighted[b % 16, pl.ds(base + b // 16 * 16, ROWS_OUT), :])
-            return total + jnp.dot(
-                jnp.concatenate(shifted, axis=1), jnp.concatenate(picks, axis=0), preferred_element_type=F32
-            )
-
-        if CHAIN < LAGS:
-            beam = lax.fori_loop(0, LAGS // CHAIN, add, jnp.zeros((ROWS_OUT, 256), F32))
-        else:
-            beam = add(0, 0.0)
-        beam = jnp.where(inside, beam, 0.0)
-        squared = jnp.sum(beam * beam, axis=0, keepdims=True)
-        power[group, 0] = squared[:, :128]
-        power[group, 1] = squared[:, 128:]
-        return carry
-
-    lax.fori_loop(0, 4, one, 0)
+        part = opened[j].T.astype(jnp.int32)
+        for h in range(2):
+            for row in range(0, ST, 8):
+                entry = table[ST * j + row : ST * j + row + 8, :]
+                index = part[ST * h + row : ST * h + row + 8]
+                for k in range(2):
+                    found = [
+                        jnp.take_along_axis(entry, index[:, c : c + 128] + k, axis=1, mode="promise_in_bounds")
+                        for c in range(0, 512, 128)
+                    ]
+                    extra[h][k] = extra[h][k] + jnp.concatenate(found, axis=1)
+    for t in range(2):
+        one, two = opened[2 * t], opened[2 * t + 1]
+        lagged[0:512, 128 * t : 128 * t + 128] = jnp.where(left, one, pltpu.roll(two, ST, 1)).astype(BF16)
+        lagged[512:, 128 * t : 128 * t + 128] = jnp.where(left, pltpu.roll(one, ST, 1), two).astype(BF16)
+    start = jnp.where(src == middle, W - (BLK * middle - HALO), 0)
+    stop = jnp.where(src == middle - 1, W - BLK * (middle - 1), jnp.where(src == SRC - 1, BLK - 1, BLK))
+    at = lax.broadcasted_iota(jnp.int32, (1, 256), 1)
+    inside = jnp.logical_and(at >= start, at < stop)
+    lag = lagged[...]
+    picks = [jnp.where(lag == BF16(b), BF16(1), BF16(0)) for b in range(LAGS)]
+    shifted = [weighted[b % COPIES, b - b % COPIES : b - b % COPIES + 256, :] for b in range(LAGS)]
+    beam = lax.dot_general(
+        jnp.concatenate(picks, axis=1),
+        jnp.concatenate(shifted, axis=1),
+        (((1,), (1,)), ((), ())),
+        preferred_element_type=F32,
+    )
+    beam = jnp.where(inside, beam, 0.0)
+    squared = beam * beam
+    squared = jnp.sum((squared[:, :128] + squared[:, 128:]).T, axis=0, keepdims=True)
+    for h in range(2):
+        row = squared[:, 512 * h : 512 * h + 512]
+        for k in range(2):
+            late = jnp.sum(extra[h][k], axis=0, keepdims=True)
+            row = row + jnp.where(256 + k < stop, late * late, 0.0)
+        for g in range(4):
+            power[4 * h + g : 4 * h + g + 1, :] = row[:, 128 * g : 128 * g + 128]
 
 
 def finish(parts, out, sums):
@@ -216,16 +220,16 @@
     far_halo = lax.ppermute(far, "src", [(middle, middle - 1), (middle - 1, middle)])
     power = call(
         beams,
-        shape((4, 2, 1, 128)),
+        shape((8, 128)),
         [VMEM] * 4,
         [
-            pltpu.VMEM((ROWS_IN, STATIONS), F32),
-            pltpu.VMEM((16, ROWS_OUT + 48, STATIONS), BF16),
-            pltpu.VMEM((4, STATIONS, 256), BF16),
-            pltpu.VMEM((512, 128), F32),
+            pltpu.VMEM((384, STATIONS), F32),
+            pltpu.VMEM((COPIES, 256 + LAGS - COPIES, STATIONS), BF16),
+            pltpu.VMEM((STATIONS, 128), F32),
+            pltpu.VMEM((1024, STATIONS), BF16),
+            pltpu.VMEM((STA, 512, 128), F32),
         ],
     )(received, main, halo, far_halo)
-    power = power.reshape(8, 128)
     parts = lax.all_to_all(jnp.broadcast_to(power[None], (DEV, 8, 128)), ("src", "sta"), 0, 0, tiled=True)
     return call(finish, shape((STEPS, CPD)), [VMEM], [pltpu.VMEM((32, 128), F32)])(parts)
 

time: 73.3 us -> 71.6 us (0.977)
  Pallas kernels: 13.2 us -> 11.6 us
    pallas_call x1, Pallas kernels: 11.1 us -> 9.45 us  [program(): call(beams, shape((8, 128)), [VMEM] * 4, [pltpu.VMEM((384, STATIONS), F32...]
where the time goes in v6:
time: 71.6 us; the launch traced here: 70.7 us
  blocking collectives  28.7 us (40%)
  waiting for transfers between devices  14.7 us (21%)
  starting transfers between devices  14.4 us (20%)
  Pallas kernels  11.6 us (16%)
  local copies, waits for them, and re-layouts  1.17 us (2%)
    all_to_all x1, blocking collectives, program(): lax.all_to_all(jnp.broadcast_to(power[None], (DEV, 8, 128)), ('src', 'sta...  28.7 us
    all_to_all x1, starting transfers between devices, program(): received = lax.all_to_all(chunks, ('src', 'sta'), 0, 0, tiled=True)  11.2 us
    ppermute x3, waiting for transfers between devices, program(): lax.ppermute(own, 'sta', [((j + k) % STA, j) for j in range(STA)])  10.5 us
    pallas_call x1, Pallas kernels, program(): call(beams, shape((8, 128)), [VMEM] * 4, [pltpu.VMEM((384, STATIONS), F32...  9.45 us
    ppermute x1, waiting for transfers between devices, program(): halo = lax.ppermute(near, 'src', pairs)  4.19 us
  transfers between devices with their start and end apart: 6, of which 3 were waited for; matrix products, arithmetic and copies ran while one was open for 0% of the time, Pallas kernels for 0%

profile of v6, /device:TPU:0, one launch (start us, length us, event | category | flops | bytes accessed | tf_op | source)
XLA Modules:
  0.0 70.7 jit_solution(18110277595715898890)
XLA Ops:
  0.0 1.2 %shard_map.46 = (f32[64,384]{1,0:T(8,128)S(1)}, bf16[4,2,1152]{2,1,0:T(2,128)(2,1)S(1)}) custom-call(f32[64,258]{1,0:T(8,128)} %trace.1, f32[64,258]{1,0:T(8,128)} %quad.1, f32[1,64]{1,0:T(1,128)} %bitcast.4, s32[64,128]{1,0:T(8,128)} %bitcast.3), custom_call_target="tpu_custom_call" | custom-call | tf_op jit(solution)/shard_map/pallas_call | solution.py:194
  1.2 1.1 %broadcast_in_dim.7 = bf16[32,4,2,1152]{3,2,1,0:T(2,128)(2,1)} broadcast(bf16[4,2,1152]{2,1,0:T(2,128)(2,1)S(1)} %get-tuple-element.10), dimensions={1,2,3} | broadcast | bytes 608256 | tf_op jit(solution)/shard_map/broadcast_in_dim | solution.py:209
  2.4 11.2 %all-to-all-start = ((bf16[128,2,1152]{2,1,0:T(2,128)(2,1)}), bf16[128,2,1152]{2,1,0:T(2,128)(2,1)S(1)}, u32[]{:S(2)}, u32[]{:S(2)}) async-start(bf16[128,2,1152]{2,1,0:T(2,128)(2,1)} %bitcast.2), calls=%async_computation | async-start | bytes 1179648 | tf_op jit(solution)/shard_map/all_to_all | solution.py:210
  13.5 0.7 %collective-permute-start = (f32[64,384]{1,0:T(8,128)S(1)}, f32[64,384]{1,0:T(8,128)S(1)}, u32[]{:S(2)}, u32[]{:S(2)}) collective-permute-start(f32[64,384]{1,0:T(8,128)S(1)} %get-tuple-element.11.e0), channel_id=1, source_target_pairs={{1,0},{2,1},{3,2},{0,3},{5,4},{6,5},{7,6},{4,7},{9,8},{10,9},{11,1... | collective-permute-start | bytes 294920 | tf_op jit(solution)/shard_map/ppermute | solution.py:208
  14.3 0.4 collective-permute-start.1
  14.7 0.1 collective-permute-start.2
  14.8 7.4 %collective-permute-done.e1 = f32[64,384]{1,0:T(8,128)S(1)} collective-permute-done((f32[64,384]{1,0:T(8,128)S(1)}, f32[64,384]{1,0:T(8,128)S(1)}, u32[]{:S(2)}, u32[]{:S(2)}) %collective-permute-start) | collective-permute-done | bytes 98336 | tf_op jit(solution)/shard_map/ppermute | solution.py:208
  22.2 3.1 %collective-permute-done.1.e2 = f32[64,384]{1,0:T(8,128)S(1)} collective-permute-done((f32[64,384]{1,0:T(8,128)S(1)}, f32[64,384]{1,0:T(8,128)S(1)}, u32[]{:S(2)}, u32[]{:S(2)}) %collective-permute-start.1) | collective-permute-done | bytes 98336 | tf_op jit(solution)/shard_map/ppermute | solution.py:208
  25.3 0.0 collective-permute-done.2.e3
  25.3 0.2 shard_map.47
  25.6 1.3 %collective-permute-start.3 = (f32[64,256]{1,0:T(8,128)S(1)}, f32[64,256]{1,0:T(8,128)S(1)}, u32[]{:S(2)}, u32[]{:S(2)}) collective-permute-start(f32[64,256]{1,0:T(8,128)S(1)} %get-tuple-element.13), channel_id=1, source_target_pairs={{4,0},{8,4},{12,8},{16,12},{20,16},{24,20},{28,24},{32,28},{36,32}... | collective-permute-start | bytes 196616 | tf_op jit(solution)/shard_map/ppermute | solution.py:219
  26.9 0.7 collective-permute-start.4
  27.5 4.2 %collective-permute-done.3.halo = f32[64,256]{1,0:T(8,128)S(1)} collective-permute-done((f32[64,256]{1,0:T(8,128)S(1)}, f32[64,256]{1,0:T(8,128)S(1)}, u32[]{:S(2)}, u32[]{:S(2)}) %collective-permute-start.3) | collective-permute-done | bytes 65568 | tf_op jit(solution)/shard_map/ppermute | solution.py:219
  31.7 0.0 collective-permute-done.4.far_halo
  31.7 0.0 all-to-all-done.received
  31.7 9.5 %shard_map.48 = f32[8,128]{1,0:T(8,128)S(1)} custom-call(bf16[128,2,1152]{2,1,0:T(2,128)(2,1)S(1)} %all-to-all-done.received, f32[384,256]{1,0:T(8,128)S(1)} %get-tuple-element.12.main, f32[64,256]{1,0:T(8,128)S(1)} %collective-permute-done.3.halo, f32[64,256]{1,0:T(8,128)S(1)} %collective-permute-done.4.far_halo), custom_call_target="tpu_custom_call" | custom-call | tf_op jit(solution)/shard_map/pallas_call | solution.py:221
  41.2 28.7 %all_to_all.10.parts = f32[128,8,128]{2,1,0:T(8,128)S(1)} all-to-all(f32[128,8,128]{2,1,0:T(8,128)S(1)} %broadcast_in_dim.8), channel_id=1, replica_groups=mesh['src'=32,'sta'=4] {'src','sta'}, dimensions={0} | all-to-all | bytes 1048576 | tf_op jit(solution)/shard_map/all_to_all | solution.py:233
  70.0 0.7 %shard_map.49 = f32[2,128]{1,0:T(2,128)} custom-call(f32[128,8,128]{2,1,0:T(8,128)S(1)} %all_to_all.10.parts), custom_call_target="tpu_custom_call" | custom-call | tf_op jit(solution)/shard_map/pallas_call | solution.py:234
  (1 shorter events, 0.0 us)
Async XLA Ops:
  2.4 29.4 %all-to-all-start = ((bf16[128,2,1152]{2,1,0:T(2,128)(2,1)}), bf16[128,2,1152]{2,1,0:T(2,128)(2,1)S(1)}, u32[]{:S(2)}, u32[]{:S(2)}) async-start(bf16[128,2,1152]{2,1,0:T(2,128)(2,1)} %bitcast.2), calls=%async_computation | async-start | bytes 1179648 | tf_op jit(solution)/shard_map/all_to_all | solution.py:210
  13.5 8.7 %collective-permute-start = (f32[64,384]{1,0:T(8,128)S(1)}, f32[64,384]{1,0:T(8,128)S(1)}, u32[]{:S(2)}, u32[]{:S(2)}) collective-permute-start(f32[64,384]{1,0:T(8,128)S(1)} %get-tuple-element.11.e0), channel_id=1, source_target_pairs={{1,0},{2,1},{3,2},{0,3},{5,4},{6,5},{7,6},{4,7},{9,8},{10,9},{11,1... | collective-permute-start | bytes 294920 | tf_op jit(solution)/shard_map/ppermute | solution.py:208
  14.3 11.0 %collective-permute-start.1 = (f32[64,384]{1,0:T(8,128)S(1)}, f32[64,384]{1,0:T(8,128)S(1)}, u32[]{:S(2)}, u32[]{:S(2)}) collective-permute-start(f32[64,384]{1,0:T(8,128)S(1)} %get-tuple-element.11.e0), channel_id=1, source_target_pairs={{2,0},{3,1},{0,2},{1,3},{6,4},{7,5},{4,6},{5,7},{10,8},{11,9},{8,1... | collective-permute-start | bytes 294920 | tf_op jit(solution)/shard_map/ppermute | solution.py:208
  14.7 10.7 %collective-permute-start.2 = (f32[64,384]{1,0:T(8,128)S(1)}, f32[64,384]{1,0:T(8,128)S(1)}, u32[]{:S(2)}, u32[]{:S(2)}) collective-permute-start(f32[64,384]{1,0:T(8,128)S(1)} %get-tuple-element.11.e0), channel_id=1, source_target_pairs={{3,0},{0,1},{1,2},{2,3},{7,4},{4,5},{5,6},{6,7},{11,8},{8,9},{9,10... | collective-permute-start | bytes 294920 | tf_op jit(solution)/shard_map/ppermute | solution.py:208
  25.6 6.2 %collective-permute-start.3 = (f32[64,256]{1,0:T(8,128)S(1)}, f32[64,256]{1,0:T(8,128)S(1)}, u32[]{:S(2)}, u32[]{:S(2)}) collective-permute-start(f32[64,256]{1,0:T(8,128)S(1)} %get-tuple-element.13), channel_id=1, source_target_pairs={{4,0},{8,4},{12,8},{16,12},{20,16},{24,20},{28,24},{32,28},{36,32}... | collective-permute-start | bytes 196616 | tf_op jit(solution)/shard_map/ppermute | solution.py:219
  26.9 4.9 %collective-permute-start.4 = (f32[64,256]{1,0:T(8,128)S(1)}, f32[64,256]{1,0:T(8,128)S(1)}, u32[]{:S(2)}, u32[]{:S(2)}) collective-permute-start(f32[64,256]{1,0:T(8,128)S(1)} %get-tuple-element.14), channel_id=1, source_target_pairs={{64,60},{60,64},{65,61},{61,65},{66,62},{62,66},{67,63},{63,67}} | collective-permute-start | bytes 196616 | tf_op jit(solution)/shard_map/ppermute | solution.py:220

commit v7 on v6

--- a/solution.py
+++ b/solution.py
@@ -61,7 +61,7 @@
 
 def turn(e0, e1, e2, e3, main, near, far, tall):
     for k, e in enumerate((e0, e1, e2, e3)):
-        at = pl.multiple_of((lax.axis_index("sta") + k) % STA * ST, ST)
+        at = pl.multiple_of((lax.axis_index("sta") ^ k) * ST, ST)
         tall[pl.ds(at, ST), :] = e[...]
     main[...] = tall[...].T
     first, last = main[0:64, :], main[BLK - 64 : BLK, :]
@@ -153,6 +153,7 @@
 
 def finish(parts, out, sums):
     src = lax.axis_index("src")
+    h = lax.axis_index("sta") % 2
     lane = lax.broadcasted_iota(jnp.int32, (1, 128), 1)
     for k in range(STEPS):
         peak = None
@@ -160,17 +161,17 @@
             acc = parts[k * HALF + j]
             for i in range(1, SRC // STEPS):
                 acc = acc + parts[k * HALF + STA * i + j]
-            sums[8 * j : 8 * j + 8, :] = acc
+            sums[8 * j : 8 * j + 4, :] = acc
             peak = acc if peak is None else jnp.maximum(peak, acc)
         peak = jnp.max(peak, axis=(0, 1), keepdims=True)
         cells = jnp.zeros((1, 128), F32)
         for j in range(STA):
-            for h in range(2):
-                row = sums[pl.ds(8 * j + 4 * h + src // 8, 1), :]
-                to = 32 * j + 16 * h
-                row = pltpu.roll(row, (to - 16 * (src % 8)) % 128, 1)
-                cells = jnp.where(lane // 16 == to // 16, row, cells)
-        out[k : k + 1, :] = cells / peak
+            row = sums[pl.ds(8 * j + src // 8, 1), :]
+            to = 32 * j + 16 * h
+            row = pltpu.roll(row, (to - 16 * (src % 8) + 128) % 128, 1)
+            cells = jnp.where(lane // 16 == 2 * j + h, row, cells)
+        out[k : k + 1, :] = cells
+        out[STEPS + k : STEPS + k + 1, :] = jnp.broadcast_to(peak, (1, 128))
 
 
 def call(kernel, out_shape, specs, scratch=()):
@@ -205,7 +206,7 @@
     )(*inputs)
     blocks = [own]
     for k in range(1, STA):
-        blocks.append(lax.ppermute(own, "sta", [((j + k) % STA, j) for j in range(STA)]))
+        blocks.append(lax.ppermute(own, "sta", [(j ^ k, j) for j in range(STA)]))
     chunks = jnp.broadcast_to(chunk[None], (SRC, STA, 2, WIDE)).reshape(DEV, 2, WIDE)
     received = lax.all_to_all(chunks, ("src", "sta"), 0, 0, tiled=True)
     main, near, far = call(
@@ -230,8 +231,12 @@
             pltpu.VMEM((STA, 512, 128), F32),
         ],
     )(received, main, halo, far_halo)
-    parts = lax.all_to_all(jnp.broadcast_to(power[None], (DEV, 8, 128)), ("src", "sta"), 0, 0, tiled=True)
-    return call(finish, shape((STEPS, CPD)), [VMEM], [pltpu.VMEM((32, 128), F32)])(parts)
+    halves = jnp.broadcast_to(power.reshape(1, 2, 4, 128), (DEV // 2, 2, 4, 128)).reshape(DEV, 4, 128)
+    parts = lax.all_to_all(halves, ("src", "sta"), 0, 0, tiled=True)
+    mine = call(finish, shape((2 * STEPS, CPD)), [VMEM], [pltpu.VMEM((32, 128), F32)])(parts)
+    other = lax.ppermute(mine, "sta", [(0, 1), (1, 0), (2, 3), (3, 2)])
+    cells = mine[:STEPS] + other[:STEPS]
+    return cells / jnp.maximum(mine[STEPS:], other[STEPS:])
 
 
 def solution(mesh):

time: 71.6 us -> 69.8 us (0.975)
  blocking collectives: 28.7 us -> 25.5 us
  starting transfers between devices: 14.4 us -> 15.2 us
    all_to_all x1, blocking collectives: 28.7 us -> 25.5 us  [program(): parts = lax.all_to_all(halves, ('src', 'sta'), 0, 0, tiled=True)]
    ppermute x3 -> x4, starting transfers between devices: 1.26 us -> 2.11 us  [the longest x3 1.93 us: program(): blocks.append(lax.ppermute(own, 'sta', [(j ^ k, j) for j in range(STA)]))]
    ppermute x3 -> x4, waiting for transfers between devices: 10.5 us -> 10.3 us  [the longest x3 9.27 us: program(): blocks.append(lax.ppermute(own, 'sta', [(j ^ k, j) for j in range(STA)]))]
  transfers between devices with their start and end apart: 6 -> 7, of which waited for: 3 -> 4; matrix products, arithmetic and copies ran while one was open for 0% -> 0% of each run, Pallas kernels for 0% -> 0%
where the time goes in v7:
time: 69.8 us; the launch traced here: 68.5 us
  blocking collectives  25.5 us (37%)
  starting transfers between devices  15.2 us (22%)
  waiting for transfers between devices  15 us (21%)
  Pallas kernels  11 us (16%)
  local copies, waits for them, and re-layouts  1.16 us (2%)
    all_to_all x1, blocking collectives, program(): parts = lax.all_to_all(halves, ('src', 'sta'), 0, 0, tiled=True)  25.5 us
    all_to_all x1, starting transfers between devices, program(): received = lax.all_to_all(chunks, ('src', 'sta'), 0, 0, tiled=True)  11.2 us
    pallas_call x1, Pallas kernels, program(): call(beams, shape((8, 128)), [VMEM] * 4, [pltpu.VMEM((384, STATIONS), F32...  9.45 us
    ppermute x3, waiting for transfers between devices, program(): blocks.append(lax.ppermute(own, 'sta', [(j ^ k, j) for j in range(STA)]))  9.27 us
    ppermute x1, waiting for transfers between devices, program(): halo = lax.ppermute(near, 'src', pairs)  4.61 us
    ppermute x3, starting transfers between devices, program(): blocks.append(lax.ppermute(own, 'sta', [(j ^ k, j) for j in range(STA)]))  1.93 us
  transfers between devices with their start and end apart: 7, of which 4 were waited for; matrix products, arithmetic and copies ran while one was open for 0% of the time, Pallas kernels for 0%

profile of v7, /device:TPU:0, one launch (start us, length us, event | category | flops | bytes accessed | tf_op | source)
XLA Modules:
  0.0 68.5 jit_solution(4419615997570674947)
XLA Ops:
  0.0 1.2 %shard_map.46 = (f32[64,384]{1,0:T(8,128)S(1)}, bf16[4,2,1152]{2,1,0:T(2,128)(2,1)S(1)}) custom-call(f32[64,258]{1,0:T(8,128)} %trace.1, f32[64,258]{1,0:T(8,128)} %quad.1, f32[1,64]{1,0:T(1,128)} %bitcast.8, s32[64,128]{1,0:T(8,128)} %bitcast.7), custom_call_target="tpu_custom_call" | custom-call | tf_op jit(solution)/shard_map/pallas_call | solution.py:195
  1.2 1.1 %broadcast_in_dim.17 = bf16[32,4,2,1152]{3,2,1,0:T(2,128)(2,1)} broadcast(bf16[4,2,1152]{2,1,0:T(2,128)(2,1)S(1)} %get-tuple-element.10), dimensions={1,2,3} | broadcast | bytes 608256 | tf_op jit(solution)/shard_map/broadcast_in_dim | solution.py:210
  2.4 11.2 %all-to-all-start = ((bf16[128,2,1152]{2,1,0:T(2,128)(2,1)}), bf16[128,2,1152]{2,1,0:T(2,128)(2,1)S(1)}, u32[]{:S(2)}, u32[]{:S(2)}) async-start(bf16[128,2,1152]{2,1,0:T(2,128)(2,1)} %bitcast.2), calls=%async_computation | async-start | bytes 1179648 | tf_op jit(solution)/shard_map/all_to_all | solution.py:211
  13.5 0.1 collective-permute-start
  13.6 1.1 %collective-permute-start.1 = (f32[64,384]{1,0:T(8,128)S(1)}, f32[64,384]{1,0:T(8,128)S(1)}, u32[]{:S(2)}, u32[]{:S(2)}) collective-permute-start(f32[64,384]{1,0:T(8,128)S(1)} %get-tuple-element.11.e0), channel_id=1, source_target_pairs={{2,0},{3,1},{0,2},{1,3},{6,4},{7,5},{4,6},{5,7},{10,8},{11,9},{8,1... | collective-permute-start | bytes 294920 | tf_op jit(solution)/shard_map/ppermute | solution.py:209
  14.7 0.8 %collective-permute-start.2 = (f32[64,384]{1,0:T(8,128)S(1)}, f32[64,384]{1,0:T(8,128)S(1)}, u32[]{:S(2)}, u32[]{:S(2)}) collective-permute-start(f32[64,384]{1,0:T(8,128)S(1)} %get-tuple-element.11.e0), channel_id=1, source_target_pairs={{3,0},{2,1},{1,2},{0,3},{7,4},{6,5},{5,6},{4,7},{11,8},{10,9},{9,1... | collective-permute-start | bytes 294920 | tf_op jit(solution)/shard_map/ppermute | solution.py:209
  15.5 0.0 collective-permute-done.e1
  15.5 8.3 %collective-permute-done.1.e2 = f32[64,384]{1,0:T(8,128)S(1)} collective-permute-done((f32[64,384]{1,0:T(8,128)S(1)}, f32[64,384]{1,0:T(8,128)S(1)}, u32[]{:S(2)}, u32[]{:S(2)}) %collective-permute-start.1) | collective-permute-done | bytes 98336 | tf_op jit(solution)/shard_map/ppermute | solution.py:209
  23.8 1.0 %collective-permute-done.2.e3 = f32[64,384]{1,0:T(8,128)S(1)} collective-permute-done((f32[64,384]{1,0:T(8,128)S(1)}, f32[64,384]{1,0:T(8,128)S(1)}, u32[]{:S(2)}, u32[]{:S(2)}) %collective-permute-start.2) | collective-permute-done | bytes 98336 | tf_op jit(solution)/shard_map/ppermute | solution.py:209
  24.8 0.2 shard_map.47
  25.0 1.3 %collective-permute-start.3 = (f32[64,256]{1,0:T(8,128)S(1)}, f32[64,256]{1,0:T(8,128)S(1)}, u32[]{:S(2)}, u32[]{:S(2)}) collective-permute-start(f32[64,256]{1,0:T(8,128)S(1)} %get-tuple-element.13), channel_id=1, source_target_pairs={{4,0},{8,4},{12,8},{16,12},{20,16},{24,20},{28,24},{32,28},{36,32}... | collective-permute-start | bytes 196616 | tf_op jit(solution)/shard_map/ppermute | solution.py:220
  26.3 0.7 collective-permute-start.4
  26.9 4.6 %collective-permute-done.3.halo = f32[64,256]{1,0:T(8,128)S(1)} collective-permute-done((f32[64,256]{1,0:T(8,128)S(1)}, f32[64,256]{1,0:T(8,128)S(1)}, u32[]{:S(2)}, u32[]{:S(2)}) %collective-permute-start.3) | collective-permute-done | bytes 65568 | tf_op jit(solution)/shard_map/ppermute | solution.py:220
  31.6 0.0 collective-permute-done.4.far_halo
  31.6 0.0 all-to-all-done.received
  31.6 9.5 %shard_map.48 = f32[8,128]{1,0:T(8,128)S(1)} custom-call(bf16[128,2,1152]{2,1,0:T(2,128)(2,1)S(1)} %all-to-all-done.received, f32[384,256]{1,0:T(8,128)S(1)} %get-tuple-element.12.main, f32[64,256]{1,0:T(8,128)S(1)} %collective-permute-done.3.halo, f32[64,256]{1,0:T(8,128)S(1)} %collective-permute-done.4.far_halo), custom_call_target="tpu_custom_call" | custom-call | tf_op jit(solution)/shard_map/pallas_call | solution.py:222
  41.1 25.5 %all_to_all.10.parts = f32[128,4,128]{2,1,0:T(4,128)S(1)} all-to-all(f32[128,4,128]{2,1,0:T(4,128)S(1)} %bitcast.6), channel_id=1, replica_groups=mesh['src'=32,'sta'=4] {'src','sta'}, dimensions={0} | all-to-all | bytes 524288 | tf_op jit(solution)/shard_map/all_to_all | solution.py:235
  66.6 0.1 shard_map.49
  66.7 0.2 collective-permute-start.5
  66.9 1.1 %collective-permute-done.5 = f32[4,128]{1,0:T(4,128)S(1)} collective-permute-done((f32[4,128]{1,0:T(4,128)S(1)}, f32[4,128]{1,0:T(4,128)S(1)}, u32[]{:S(2)}, u32[]{:S(2)}) %collective-permute-start.5) | collective-permute-done | bytes 2080 | tf_op jit(solution)/shard_map/ppermute | solution.py:237
  68.0 0.6 maximum_divide_fusion
  (1 shorter events, 0.0 us)
Async XLA Ops:
  2.4 29.2 %all-to-all-start = ((bf16[128,2,1152]{2,1,0:T(2,128)(2,1)}), bf16[128,2,1152]{2,1,0:T(2,128)(2,1)S(1)}, u32[]{:S(2)}, u32[]{:S(2)}) async-start(bf16[128,2,1152]{2,1,0:T(2,128)(2,1)} %bitcast.2), calls=%async_computation | async-start | bytes 1179648 | tf_op jit(solution)/shard_map/all_to_all | solution.py:211
  13.5 1.9 %collective-permute-start = (f32[64,384]{1,0:T(8,128)S(1)}, f32[64,384]{1,0:T(8,128)S(1)}, u32[]{:S(2)}, u32[]{:S(2)}) collective-permute-start(f32[64,384]{1,0:T(8,128)S(1)} %get-tuple-element.11.e0), channel_id=1, source_target_pairs={{1,0},{0,1},{3,2},{2,3},{5,4},{4,5},{7,6},{6,7},{9,8},{8,9},{11,10... | collective-permute-start | bytes 294920 | tf_op jit(solution)/shard_map/ppermute | solution.py:209
  13.6 10.2 %collective-permute-start.1 = (f32[64,384]{1,0:T(8,128)S(1)}, f32[64,384]{1,0:T(8,128)S(1)}, u32[]{:S(2)}, u32[]{:S(2)}) collective-permute-start(f32[64,384]{1,0:T(8,128)S(1)} %get-tuple-element.11.e0), channel_id=1, source_target_pairs={{2,0},{3,1},{0,2},{1,3},{6,4},{7,5},{4,6},{5,7},{10,8},{11,9},{8,1... | collective-permute-start | bytes 294920 | tf_op jit(solution)/shard_map/ppermute | solution.py:209
  14.7 10.1 %collective-permute-start.2 = (f32[64,384]{1,0:T(8,128)S(1)}, f32[64,384]{1,0:T(8,128)S(1)}, u32[]{:S(2)}, u32[]{:S(2)}) collective-permute-start(f32[64,384]{1,0:T(8,128)S(1)} %get-tuple-element.11.e0), channel_id=1, source_target_pairs={{3,0},{2,1},{1,2},{0,3},{7,4},{6,5},{5,6},{4,7},{11,8},{10,9},{9,1... | collective-permute-start | bytes 294920 | tf_op jit(solution)/shard_map/ppermute | solution.py:209
  25.0 6.6 %collective-permute-start.3 = (f32[64,256]{1,0:T(8,128)S(1)}, f32[64,256]{1,0:T(8,128)S(1)}, u32[]{:S(2)}, u32[]{:S(2)}) collective-permute-start(f32[64,256]{1,0:T(8,128)S(1)} %get-tuple-element.13), channel_id=1, source_target_pairs={{4,0},{8,4},{12,8},{16,12},{20,16},{24,20},{28,24},{32,28},{36,32}... | collective-permute-start | bytes 196616 | tf_op jit(solution)/shard_map/ppermute | solution.py:220
  26.3 5.3 %collective-permute-start.4 = (f32[64,256]{1,0:T(8,128)S(1)}, f32[64,256]{1,0:T(8,128)S(1)}, u32[]{:S(2)}, u32[]{:S(2)}) collective-permute-start(f32[64,256]{1,0:T(8,128)S(1)} %get-tuple-element.14), channel_id=1, source_target_pairs={{64,60},{60,64},{65,61},{61,65},{66,62},{62,66},{67,63},{63,67}} | collective-permute-start | bytes 196616 | tf_op jit(solution)/shard_map/ppermute | solution.py:221
  66.7 1.2 %collective-permute-start.5 = (f32[4,128]{1,0:T(4,128)S(1)}, f32[4,128]{1,0:T(4,128)S(1)}, u32[]{:S(2)}, u32[]{:S(2)}) collective-permute-start(f32[4,128]{1,0:T(4,128)S(1)} %shard_map.49), channel_id=1, source_target_pairs={{0,1},{1,0},{2,3},{3,2},{4,5},{5,4},{6,7},{7,6},{8,9},{9,8},{10,11... | collective-permute-start | bytes 6152 | tf_op jit(solution)/shard_map/ppermute | solution.py:237

commit v8 on v7

--- a/solution.py
+++ b/solution.py
@@ -20,7 +20,7 @@
 ST = 64
 STATIONS = ST * STA
 HALO = LAGS - 1
-COPIES = 16
+COPIES = 8
 CPD = 128
 WIDE = 9 * 128
 SAMPLES = BLK * SRC
@@ -34,7 +34,10 @@
     ]
     for copy in copies:
         copy.start()
-    for copy in copies:
+    copies[3].wait()
+    lag = lg_in[...].astype(F32)
+    lag = jnp.concatenate([lag, lag], axis=0).T
+    for copy in copies[:3]:
         copy.wait()
     tr, qd = tr_in[...], qd_in[...]
     energy = tr * tr + qd * qd
@@ -51,8 +54,6 @@
     row = lax.broadcasted_iota(jnp.int32, (2, 128), 0)
     lane = lax.broadcasted_iota(jnp.int32, (2, 128), 1)
     sums = jnp.where(row == 0, jnp.where(lane < ST, hi, mid), jnp.where(lane < ST, low, 0.0))
-    lag = lg_in[...].astype(F32)
-    lag = jnp.concatenate([lag, lag], axis=0).T
     for j in range(STA):
         body = jnp.where(lane[:1] < ST, lag[32 * j : 32 * j + 16], lag[32 * j + 16 : 32 * j + 32])
         pieces = [body[2 * k : 2 * k + 2] for k in range(8)] + [sums]

time: 69.8 us -> 69.8 us (level)
  no operation moved by 1% of the time
where the time goes in v8:
time: 69.8 us; the launch traced here: 68.6 us
  blocking collectives  25.5 us (37%)
  starting transfers between devices  15.2 us (22%)
  waiting for transfers between devices  15 us (21%)
  Pallas kernels  11.1 us (16%)
  local copies, waits for them, and re-layouts  1.16 us (2%)
    all_to_all x1, blocking collectives, program(): parts = lax.all_to_all(halves, ('src', 'sta'), 0, 0, tiled=True)  25.5 us
    all_to_all x1, starting transfers between devices, program(): received = lax.all_to_all(chunks, ('src', 'sta'), 0, 0, tiled=True)  11.2 us
    pallas_call x1, Pallas kernels, program(): call(beams, shape((8, 128)), [VMEM] * 4, [pltpu.VMEM((384, STATIONS), F32...  9.45 us
    ppermute x3, waiting for transfers between devices, program(): blocks.append(lax.ppermute(own, 'sta', [(j ^ k, j) for j in range(STA)]))  9.27 us
    ppermute x1, waiting for transfers between devices, program(): halo = lax.ppermute(near, 'src', pairs)  4.61 us
    ppermute x3, starting transfers between devices, program(): blocks.append(lax.ppermute(own, 'sta', [(j ^ k, j) for j in range(STA)]))  1.93 us
  transfers between devices with their start and end apart: 7, of which 4 were waited for; matrix products, arithmetic and copies ran while one was open for 0% of the time, Pallas kernels for 0%

profile of v8, /device:TPU:0, one launch (start us, length us, event | category | flops | bytes accessed | tf_op | source)
XLA Modules:
  0.0 68.6 jit_solution(3259950456606032753)
XLA Ops:
  0.0 1.3 %shard_map.46 = (f32[64,384]{1,0:T(8,128)S(1)}, bf16[4,2,1152]{2,1,0:T(2,128)(2,1)S(1)}) custom-call(f32[64,258]{1,0:T(8,128)} %trace.1, f32[64,258]{1,0:T(8,128)} %quad.1, f32[1,64]{1,0:T(1,128)} %bitcast.8, s32[64,128]{1,0:T(8,128)} %bitcast.7), custom_call_target="tpu_custom_call" | custom-call | tf_op jit(solution)/shard_map/pallas_call | solution.py:196
  1.3 1.1 %broadcast_in_dim.17 = bf16[32,4,2,1152]{3,2,1,0:T(2,128)(2,1)} broadcast(bf16[4,2,1152]{2,1,0:T(2,128)(2,1)S(1)} %get-tuple-element.10), dimensions={1,2,3} | broadcast | bytes 608256 | tf_op jit(solution)/shard_map/broadcast_in_dim | solution.py:211
  2.4 11.2 %all-to-all-start = ((bf16[128,2,1152]{2,1,0:T(2,128)(2,1)}), bf16[128,2,1152]{2,1,0:T(2,128)(2,1)S(1)}, u32[]{:S(2)}, u32[]{:S(2)}) async-start(bf16[128,2,1152]{2,1,0:T(2,128)(2,1)} %bitcast.2), calls=%async_computation | async-start | bytes 1179648 | tf_op jit(solution)/shard_map/all_to_all | solution.py:212
  13.6 0.1 collective-permute-start
  13.7 1.1 %collective-permute-start.1 = (f32[64,384]{1,0:T(8,128)S(1)}, f32[64,384]{1,0:T(8,128)S(1)}, u32[]{:S(2)}, u32[]{:S(2)}) collective-permute-start(f32[64,384]{1,0:T(8,128)S(1)} %get-tuple-element.11.e0), channel_id=1, source_target_pairs={{2,0},{3,1},{0,2},{1,3},{6,4},{7,5},{4,6},{5,7},{10,8},{11,9},{8,1... | collective-permute-start | bytes 294920 | tf_op jit(solution)/shard_map/ppermute | solution.py:210
  14.7 0.8 %collective-permute-start.2 = (f32[64,384]{1,0:T(8,128)S(1)}, f32[64,384]{1,0:T(8,128)S(1)}, u32[]{:S(2)}, u32[]{:S(2)}) collective-permute-start(f32[64,384]{1,0:T(8,128)S(1)} %get-tuple-element.11.e0), channel_id=1, source_target_pairs={{3,0},{2,1},{1,2},{0,3},{7,4},{6,5},{5,6},{4,7},{11,8},{10,9},{9,1... | collective-permute-start | bytes 294920 | tf_op jit(solution)/shard_map/ppermute | solution.py:210
  15.5 0.0 collective-permute-done.e1
  15.5 8.3 %collective-permute-done.1.e2 = f32[64,384]{1,0:T(8,128)S(1)} collective-permute-done((f32[64,384]{1,0:T(8,128)S(1)}, f32[64,384]{1,0:T(8,128)S(1)}, u32[]{:S(2)}, u32[]{:S(2)}) %collective-permute-start.1) | collective-permute-done | bytes 98336 | tf_op jit(solution)/shard_map/ppermute | solution.py:210
  23.8 1.0 %collective-permute-done.2.e3 = f32[64,384]{1,0:T(8,128)S(1)} collective-permute-done((f32[64,384]{1,0:T(8,128)S(1)}, f32[64,384]{1,0:T(8,128)S(1)}, u32[]{:S(2)}, u32[]{:S(2)}) %collective-permute-start.2) | collective-permute-done | bytes 98336 | tf_op jit(solution)/shard_map/ppermute | solution.py:210
  24.8 0.2 shard_map.47
  25.0 1.3 %collective-permute-start.3 = (f32[64,256]{1,0:T(8,128)S(1)}, f32[64,256]{1,0:T(8,128)S(1)}, u32[]{:S(2)}, u32[]{:S(2)}) collective-permute-start(f32[64,256]{1,0:T(8,128)S(1)} %get-tuple-element.13), channel_id=1, source_target_pairs={{4,0},{8,4},{12,8},{16,12},{20,16},{24,20},{28,24},{32,28},{36,32}... | collective-permute-start | bytes 196616 | tf_op jit(solution)/shard_map/ppermute | solution.py:221
  26.3 0.7 collective-permute-start.4
  27.0 4.6 %collective-permute-done.3.halo = f32[64,256]{1,0:T(8,128)S(1)} collective-permute-done((f32[64,256]{1,0:T(8,128)S(1)}, f32[64,256]{1,0:T(8,128)S(1)}, u32[]{:S(2)}, u32[]{:S(2)}) %collective-permute-start.3) | collective-permute-done | bytes 65568 | tf_op jit(solution)/shard_map/ppermute | solution.py:221
  31.6 0.0 collective-permute-done.4.far_halo
  31.6 0.0 all-to-all-done.received
  31.6 9.4 %shard_map.48 = f32[8,128]{1,0:T(8,128)S(1)} custom-call(bf16[128,2,1152]{2,1,0:T(2,128)(2,1)S(1)} %all-to-all-done.received, f32[384,256]{1,0:T(8,128)S(1)} %get-tuple-element.12.main, f32[64,256]{1,0:T(8,128)S(1)} %collective-permute-done.3.halo, f32[64,256]{1,0:T(8,128)S(1)} %collective-permute-done.4.far_halo), custom_call_target="tpu_custom_call" | custom-call | tf_op jit(solution)/shard_map/pallas_call | solution.py:223
  41.1 25.5 %all_to_all.10.parts = f32[128,4,128]{2,1,0:T(4,128)S(1)} all-to-all(f32[128,4,128]{2,1,0:T(4,128)S(1)} %bitcast.6), channel_id=1, replica_groups=mesh['src'=32,'sta'=4] {'src','sta'}, dimensions={0} | all-to-all | bytes 524288 | tf_op jit(solution)/shard_map/all_to_all | solution.py:236
  66.6 0.1 shard_map.49
  66.8 0.2 collective-permute-start.5
  66.9 1.1 %collective-permute-done.5 = f32[4,128]{1,0:T(4,128)S(1)} collective-permute-done((f32[4,128]{1,0:T(4,128)S(1)}, f32[4,128]{1,0:T(4,128)S(1)}, u32[]{:S(2)}, u32[]{:S(2)}) %collective-permute-start.5) | collective-permute-done | bytes 2080 | tf_op jit(solution)/shard_map/ppermute | solution.py:238
  68.0 0.6 maximum_divide_fusion
  (1 shorter events, 0.0 us)
Async XLA Ops:
  2.4 29.2 %all-to-all-start = ((bf16[128,2,1152]{2,1,0:T(2,128)(2,1)}), bf16[128,2,1152]{2,1,0:T(2,128)(2,1)S(1)}, u32[]{:S(2)}, u32[]{:S(2)}) async-start(bf16[128,2,1152]{2,1,0:T(2,128)(2,1)} %bitcast.2), calls=%async_computation | async-start | bytes 1179648 | tf_op jit(solution)/shard_map/all_to_all | solution.py:212
  13.6 1.9 %collective-permute-start = (f32[64,384]{1,0:T(8,128)S(1)}, f32[64,384]{1,0:T(8,128)S(1)}, u32[]{:S(2)}, u32[]{:S(2)}) collective-permute-start(f32[64,384]{1,0:T(8,128)S(1)} %get-tuple-element.11.e0), channel_id=1, source_target_pairs={{1,0},{0,1},{3,2},{2,3},{5,4},{4,5},{7,6},{6,7},{9,8},{8,9},{11,10... | collective-permute-start | bytes 294920 | tf_op jit(solution)/shard_map/ppermute | solution.py:210
  13.7 10.2 %collective-permute-start.1 = (f32[64,384]{1,0:T(8,128)S(1)}, f32[64,384]{1,0:T(8,128)S(1)}, u32[]{:S(2)}, u32[]{:S(2)}) collective-permute-start(f32[64,384]{1,0:T(8,128)S(1)} %get-tuple-element.11.e0), channel_id=1, source_target_pairs={{2,0},{3,1},{0,2},{1,3},{6,4},{7,5},{4,6},{5,7},{10,8},{11,9},{8,1... | collective-permute-start | bytes 294920 | tf_op jit(solution)/shard_map/ppermute | solution.py:210
  14.7 10.1 %collective-permute-start.2 = (f32[64,384]{1,0:T(8,128)S(1)}, f32[64,384]{1,0:T(8,128)S(1)}, u32[]{:S(2)}, u32[]{:S(2)}) collective-permute-start(f32[64,384]{1,0:T(8,128)S(1)} %get-tuple-element.11.e0), channel_id=1, source_target_pairs={{3,0},{2,1},{1,2},{0,3},{7,4},{6,5},{5,6},{4,7},{11,8},{10,9},{9,1... | collective-permute-start | bytes 294920 | tf_op jit(solution)/shard_map/ppermute | solution.py:210
  25.0 6.6 %collective-permute-start.3 = (f32[64,256]{1,0:T(8,128)S(1)}, f32[64,256]{1,0:T(8,128)S(1)}, u32[]{:S(2)}, u32[]{:S(2)}) collective-permute-start(f32[64,256]{1,0:T(8,128)S(1)} %get-tuple-element.13), channel_id=1, source_target_pairs={{4,0},{8,4},{12,8},{16,12},{20,16},{24,20},{28,24},{32,28},{36,32}... | collective-permute-start | bytes 196616 | tf_op jit(solution)/shard_map/ppermute | solution.py:221
  26.3 5.3 %collective-permute-start.4 = (f32[64,256]{1,0:T(8,128)S(1)}, f32[64,256]{1,0:T(8,128)S(1)}, u32[]{:S(2)}, u32[]{:S(2)}) collective-permute-start(f32[64,256]{1,0:T(8,128)S(1)} %get-tuple-element.14), channel_id=1, source_target_pairs={{64,60},{60,64},{65,61},{61,65},{66,62},{62,66},{67,63},{63,67}} | collective-permute-start | bytes 196616 | tf_op jit(solution)/shard_map/ppermute | solution.py:222
  66.8 1.2 %collective-permute-start.5 = (f32[4,128]{1,0:T(4,128)S(1)}, f32[4,128]{1,0:T(4,128)S(1)}, u32[]{:S(2)}, u32[]{:S(2)}) collective-permute-start(f32[4,128]{1,0:T(4,128)S(1)} %shard_map.49), channel_id=1, source_target_pairs={{0,1},{1,0},{2,3},{3,2},{4,5},{5,4},{6,7},{7,6},{8,9},{9,8},{10,11... | collective-permute-start | bytes 6152 | tf_op jit(solution)/shard_map/ppermute | solution.py:238
